TPU v7x, 32 devices: a whole 2x2x4 slice. The times are simulated.
32 devices in a mesh: grp: 2 (over x), ord: 16 (over z, y, core).
Axes of the slice: x: 2, y: 2, z: 4, core: 2. Of those that a mesh axis runs over, the one named last changes fastest.
Arguments:
- grid: bfloat16 [1024, 1024, 256], P(('grp', 'ord')), parts along dimension 0, may hold values from -6 to 6
- legendre: bfloat16 [16, 64, 512, 512], P('ord'), as said below
- mixing: bfloat16 [512, 2, 256, 256], P('ord'), may hold values from -0.25 to 0.25
Outputs:
- spectrum: bfloat16 [1024, 512, 512], P(('grp', 'ord')), parts along dimension 0
There are 2 independent parts, one for each index of `grp`. A program takes and returns all parts, laid end to end along the dimension named above; an argument that names none is the same for every part. Nothing has to cross between parts.
Inputs may be any that keep to these rules, and one draw needn't show every extreme that they name: `legendre`: entries whose degree is below their order are zero. The slots 32 to 63 of block index b repeat the panels that block index 16 - 1 - b holds in its slots 0 to 31.
All inputs are finite; a program needn't handle non-finite values.
Results may differ from a plain program's by a relative error of at most 0.0062.
Values may be sent and summed in bfloat16 or wider, within the bound.
No kernel may reach another device: no remote copies, remote signals or barrier semaphores. Data moves between devices by JAX's collectives and lax.ppermute only.
A program may use at most 256 MiB of HBM per device.

v0:
```python
import math

import jax
import jax.numpy as jnp
from jax import lax
from jax.sharding import PartitionSpec as P

DEG_TILE = 128


def fourier_table(nlon, orders):
    longitude = jnp.arange(nlon, dtype=jnp.int32)
    order = jnp.arange(orders, dtype=jnp.int32)
    phase = longitude[:, None] * order[None, :] % nlon
    angle = phase.astype(jnp.float32) * (2.0 * math.pi / nlon)
    scale = 1.0 / math.sqrt(nlon)
    table = jnp.stack([jnp.cos(angle) * scale, -jnp.sin(angle) * scale], axis=-1)
    return table.reshape(nlon, 2 * orders).astype(jnp.bfloat16)


def legendre_tiles(panel, arrived, first):
    groups, degrees, latitudes = panel.shape
    width = arrived.shape[2]
    buffer = jnp.zeros((groups, degrees, width), jnp.float32)

    def advance(index, current):
        start = index * DEG_TILE
        piece = lax.dynamic_slice_in_dim(panel, start, DEG_TILE, 1)
        part = jnp.einsum("mlt,tmk->mlk", piece, arrived, preferred_element_type=jnp.float32)
        return lax.dynamic_update_slice_in_dim(current, part, start, 1)

    return lax.fori_loop(first, degrees // DEG_TILE, advance, buffer).astype(jnp.bfloat16)


def on_device(grid, legendre, mixing):
    count = lax.axis_size("ord")
    block = lax.axis_index("ord")
    lat_rows, nlon, chans = grid.shape
    panels = legendre[0]
    per_dev = panels.shape[0] // 2
    orders = per_dev * count
    table = fourier_table(nlon, orders)
    spectra = jnp.einsum("tnc,nk->tkc", grid, table, preferred_element_type=jnp.float32).astype(
        jnp.bfloat16
    )
    sending = spectra.reshape(lat_rows, orders, 2 * chans)
    arrived = lax.all_to_all(sending, "ord", split_axis=1, concat_axis=0, tiled=True)
    first = per_dev * block // DEG_TILE
    coeffs = legendre_tiles(panels[:per_dev], arrived, first)
    landed = lax.all_to_all(coeffs, "ord", split_axis=1, concat_axis=0, tiled=True)
    real_part = mixing[:, 0]
    imag_part = mixing[:, 1]
    block_weight = jnp.concatenate(
        [
            jnp.concatenate([real_part, imag_part], axis=-1),
            jnp.concatenate([-imag_part, real_part], axis=-1),
        ],
        axis=1,
    )
    mixed = jnp.einsum("mlk,lkn->lmn", landed, block_weight, preferred_element_type=jnp.float32)
    return mixed.astype(jnp.bfloat16)


def solution(mesh):
    return jax.shard_map(
        on_device,
        mesh=mesh,
        in_specs=(
            P(("grp", "ord"), None, None),
            P("ord", None, None, None),
            P("ord", None, None, None),
        ),
        out_specs=P(("grp", "ord"), None, None),
        check_vma=False,
    )
```

profile of v0, /device:TPU:21, one launch (start us, length us, event | category | flops | bytes accessed | tf_op | source)
XLA Modules:
  0.0 916.6 jit_solution(554978800378174407)
XLA Ops:
  0.0 8.6 multiply_convert_fusion
  8.6 0.2 pad_maximum_fusion
  8.8 3.9 copy.20
  12.8 2.7 reshape.84
  15.5 25.9 %convert_bitcast_fusion = bf16[32,1024,256]{2,1,0:T(8,128)(2,1)} fusion(bf16[1024,1024,1]{0,1,2:T(8,128)(2,1)S(1)} %reshape.84, bf16[32,1024,256]{2,1,0:T(8,128)(2,1)} %param.5), kind=kOutput, calls=%fused_computation.12 | convolution fusion | flops 17188257792 | bytes 35651584 | tf_op jit(solution)/shard_map/tnc,nk->tkc/dot_general | solution.py:43
  41.4 24.5 %reshape.83 = bf16[32,512,512]{2,1,0:T(8,128)(2,1)} reshape(bf16[32,1024,256]{2,1,0:T(8,128)(2,1)} %convert_bitcast_fusion) | data formatting | bytes 33554432 | tf_op jit(solution)/shard_map/reshape | solution.py:46
  65.9 18.5 %copy.21 = bf16[32,512,512]{2,0,1:T(8,128)(2,1)} copy(bf16[32,512,512]{2,1,0:T(8,128)(2,1)} %reshape.83) | data formatting | bytes 33554432 | tf_op jit(solution)/shard_map/reshape | solution.py:46
  84.3 6.4 all-to-all-start
  90.8 13.7 %slice_bitcast_fusion = bf16[32,512,512]{2,1,0:T(8,128)(2,1)} fusion(bf16[1,64,512,512]{3,2,1,0:T(8,128)(2,1)} %param.6), kind=kLoop, calls=%fused_computation.13 | loop fusion | bytes 33554432 | tf_op jit(solution)/shard_map/slice | solution.py:49
  104.5 346.3 %all-to-all-done = bf16[32,512,512]{2,0,1:T(8,128)(2,1)} async-done(((bf16[32,512,512]{2,0,1:T(8,128)(2,1)}), bf16[32,512,512]{2,0,1:T(8,128)(2,1)}, u32[]{:S(2)}, u32[]{:S(2)}) %all-to-all-start) | async-done | bytes 16777248 | tf_op jit(solution)/shard_map/all_to_all | solution.py:47
  450.8 14.1 %copy.22 = bf16[16,32,32,512]{3,1,0,2:T(8,128)(2,1)} copy(bf16[16,32,32,512]{3,1,2,0:T(8,128)(2,1)} %bitcast.3) | data formatting | bytes 33554432 | tf_op jit(solution)/shard_map/all_to_all | solution.py:47
  464.9 6.1 broadcast_in_dim.2.clone
  471.0 27.6 %while.10 = (s32[]{:T(128)}, bf16[32,512,512]{2,0,1:T(8,128)(2,1)}, bf16[32,512,512]{2,1,0:T(8,128)(2,1)}, bf16[512,32,512]{2,0,1:T(8,128)(2,1)}, s32[]{:T(128)}, /*index=5*/s32[]{:T(128)}, s32[]{:T(128)}, s32[]{:T(128)}) while((s32[]{:T(128)}, bf16[32,512,512]{2,0,1:T(8,128)(2,1)}, bf16[32,512,512]{2,1,0:T(8,128)(2,1)}, ...), condition=%wide.region_1.2_spmd, body=%wide.region_0.1_spmd.sunk | while | flops 2147483648 | bytes 33554568 | solution.py:32
  471.0 9.4 %fusion.31 = bf16[32,128,512]{2,1,0:T(8,128)(2,1)S(1)} fusion(bf16[512,32,512]{2,0,1:T(8,128)(2,1)} %get-tuple-element.84, bf16[32,512,512]{2,1,0:T(8,128)(2,1)} %get-tuple-element.83, s32[]{:T(128)S(6)} %select_n.40), kind=kOutput, calls=%fused_computation.1.clone.1 | convolution fusion | flops 2147483648 | bytes 25165828 | tf_op jit(solution)/shard_map/while/body/mlt,tmk->mlk/dot_general | solution.py:29
  480.4 4.4 copy_dynamic-update-slice_fusion.2
  484.8 9.4 %fusion.31 = bf16[32,128,512]{2,1,0:T(8,128)(2,1)S(1)} fusion(bf16[512,32,512]{2,0,1:T(8,128)(2,1)} %get-tuple-element.84, bf16[32,512,512]{2,1,0:T(8,128)(2,1)} %get-tuple-element.83, s32[]{:T(128)S(6)} %select_n.40), kind=kOutput, calls=%fused_computation.1.clone.1 | convolution fusion | flops 2147483648 | bytes 25165828 | tf_op jit(solution)/shard_map/while/body/mlt,tmk->mlk/dot_general | solution.py:29
  494.2 4.4 copy_dynamic-update-slice_fusion.2
  498.6 20.0 %all-to-all-start.1 = ((bf16[32,512,512]{2,0,1:T(8,128)(2,1)}), bf16[32,512,512]{2,0,1:T(8,128)(2,1)}, u32[]{:S(2)}, u32[]{:S(2)}) async-start(bf16[32,512,512]{2,0,1:T(8,128)(2,1)} %get-tuple-element.27), calls=%async_computation.1 | async-start | bytes 33554432 | tf_op jit(solution)/shard_map/all_to_all | solution.py:50
  518.5 4.4 fusion.21
  522.9 5.9 slice_bitcast_fusion.1
  528.8 349.7 %all-to-all-done.1 = bf16[32,512,512]{2,0,1:T(8,128)(2,1)} async-done(((bf16[32,512,512]{2,0,1:T(8,128)(2,1)}), bf16[32,512,512]{2,0,1:T(8,128)(2,1)}, u32[]{:S(2)}, u32[]{:S(2)}) %all-to-all-start.1) | async-done | bytes 16777248 | tf_op jit(solution)/shard_map/all_to_all | solution.py:50
  878.5 0.0 copy-start
  878.5 14.4 %copy.24 = bf16[32,16,32,512]{3,0,1,2:T(8,128)(2,1)} copy(bf16[32,16,32,512]{3,0,2,1:T(8,128)(2,1)} %bitcast.5) | data formatting | bytes 33554432 | tf_op jit(solution)/shard_map/all_to_all | solution.py:50
  892.9 0.0 copy-done
  892.9 23.6 %fusion.11 = bf16[32,512,512]{2,1,0:T(8,128)(2,1)} fusion(bf16[512,32,512]{2,0,1:T(8,128)(2,1)} %bitcast.31, bf16[32,256,256]{2,1,0:T(8,128)(2,1)} %get-tuple-element.37, bf16[32,256,256]{2,1,0:T(8,128)(2,1)S(1)} %copy-done, bf16[32,256,256]{2,1,0:T(8,128)(2,1)} %get-tuple-element.36), kind=kOutput, calls=%fused_computation.14 | convolution fusion | flops 8665432064 | bytes 46137344 | tf_op jit(solution)/shard_map/mlk,lkn->lmn/dot_general | solution.py:60
Async XLA Ops:
  84.3 366.5 %all-to-all-start = ((bf16[32,512,512]{2,0,1:T(8,128)(2,1)}), bf16[32,512,512]{2,0,1:T(8,128)(2,1)}, u32[]{:S(2)}, u32[]{:S(2)}) async-start(bf16[32,512,512]{2,0,1:T(8,128)(2,1)} %copy.21), calls=%async_computation | async-start | bytes 33554432 | tf_op jit(solution)/shard_map/all_to_all | solution.py:47
  498.6 380.0 %all-to-all-start.1 = ((bf16[32,512,512]{2,0,1:T(8,128)(2,1)}), bf16[32,512,512]{2,0,1:T(8,128)(2,1)}, u32[]{:S(2)}, u32[]{:S(2)}) async-start(bf16[32,512,512]{2,0,1:T(8,128)(2,1)} %get-tuple-element.27), calls=%async_computation.1 | async-start | bytes 33554432 | tf_op jit(solution)/shard_map/all_to_all | solution.py:50
  878.5 14.4 %copy-start = (bf16[32,256,256]{2,1,0:T(8,128)(2,1)S(1)}, bf16[32,256,256]{2,1,0:T(8,128)(2,1)}, u32[]{:S(2)}) copy-start(bf16[32,256,256]{2,1,0:T(8,128)(2,1)} %fusion.21) | copy-start | bytes 12582916
where the time goes:
time: 921 us; the launch traced here: 917 us
  waiting for transfers between devices  696 us (76%)
  local copies, waits for them, and re-layouts  113 us (12%)
  matrix products  68.3 us (7%)
  starting transfers between devices  26.4 us (3%)
  other arithmetic  13.2 us (1%)
    all_to_all x1, waiting for transfers between devices, on_device(): lax.all_to_all(coeffs, 'ord', split_axis=1, concat_axis=0, tiled=True)  350 us
    all_to_all x1, waiting for transfers between devices, on_device(): lax.all_to_all(sending, 'ord', split_axis=1, concat_axis=0, tiled=True)  346 us
    reshape x2, local copies, waits for them, and re-layouts, on_device(): sending = spectra.reshape(lat_rows, orders, 2 * chans)  43 us
    dot_general x1, matrix products, on_device(): jnp.einsum('tnc,nk->tkc', grid, table, preferred_element_type=jnp.float32)  25.9 us
    dot_general x1, matrix products, on_device(): jnp.einsum('mlk,lkn->lmn', landed, block_weight, preferred_element_type=j...  23.6 us
    all_to_all x1, starting transfers between devices, on_device(): lax.all_to_all(coeffs, 'ord', split_axis=1, concat_axis=0, tiled=True)  20 us
    dot_general x2, matrix products, advance(): jnp.einsum('mlt,tmk->mlk', piece, arrived, preferred_element_type=jnp.flo...  18.8 us
  transfers between devices with their start and end apart: 2, of which 2 were waited for; matrix products, arithmetic and copies ran while one was open for 3% of the time, Pallas kernels for 0%

commit v1 on v0

v1 whole, which is shorter than its diff:
```python
import functools
import math

import jax
import jax.numpy as jnp
import ml_dtypes
import numpy as np
from jax import lax
from jax.experimental import pallas as pl
from jax.experimental.pallas import tpu as pltpu
from jax.sharding import PartitionSpec as P

CHUNK = 8
PARTS = 2
TILE = 16
VMEM_LIMIT = 56 << 20


def fourier_table(nlon, count, per_dev, first, size):
    owner = np.arange(count)[:, None]
    order = ((count - 1 - owner) * per_dev + first + np.arange(size)[None, :]).reshape(-1)
    phase = order[:, None] * np.arange(nlon)[None, :] % nlon
    angle = phase.astype(np.float32) * np.float32(2.0 * math.pi / nlon)
    scale = np.float32(1.0 / math.sqrt(nlon))
    table = np.concatenate([np.cos(angle) * scale, -np.sin(angle) * scale], axis=0)
    return table.astype(ml_dtypes.bfloat16)


def swap_matrix(outer, inner):
    rows = np.arange(outer * inner)
    source = rows % outer * inner + rows // outer
    return (source[:, None] == rows[None, :]).astype(ml_dtypes.bfloat16)


def fourier_kernel(rows_step, table_ref, swap_ref, grid_ref, out_ref, hold):
    group, rows, chans = hold.shape
    pairs = rows // 2
    steps = group // rows_step
    part = lax.rem(pl.program_id(0), steps)
    for row in range(rows_step):
        result = jnp.dot(table_ref[...], grid_ref[row], preferred_element_type=jnp.float32)
        hold[part * rows_step + row] = result.astype(jnp.bfloat16)

    @pl.when(part == steps - 1)
    def _():
        for first in range(0, rows, TILE):
            values = hold[:, first : first + TILE, :].reshape(group * TILE, chans)
            swapped = jnp.dot(swap_ref[...], values, preferred_element_type=jnp.float32)
            p, pair = first // pairs, first % pairs
            out_ref[pair : pair + TILE, :, p * chans : (p + 1) * chans] = swapped.astype(jnp.bfloat16).reshape(
                TILE, group, chans
            )


def fourier(grid, table, count, size):
    lat_rows, nlon, chans = grid.shape
    pairs = count * size
    if lat_rows % TILE or pairs % TILE:
        result = jnp.einsum("rn,tnc->rtc", table, grid, preferred_element_type=jnp.float32).astype(jnp.bfloat16)
        result = result.reshape(2, count, size, lat_rows, chans).transpose(1, 2, 3, 0, 4)
        return result.reshape(count, size, lat_rows, 2 * chans)
    rows_step = 4
    out = pl.pallas_call(
        functools.partial(fourier_kernel, rows_step),
        out_shape=jax.ShapeDtypeStruct((pairs, lat_rows, 2 * chans), jnp.bfloat16),
        grid=(lat_rows // rows_step,),
        in_specs=[
            pl.BlockSpec(table.shape, lambda g: (0, 0)),
            pl.BlockSpec((TILE * TILE, TILE * TILE), lambda g: (0, 0)),
            pl.BlockSpec((rows_step, nlon, chans), lambda g: (g, 0, 0)),
        ],
        out_specs=pl.BlockSpec((pairs, TILE, 2 * chans), lambda g: (0, g // (TILE // rows_step), 0)),
        scratch_shapes=[pltpu.VMEM((TILE, 2 * pairs, chans), jnp.bfloat16)],
        compiler_params=pltpu.CompilerParams(vmem_limit_bytes=VMEM_LIMIT),
        cost_estimate=pl.CostEstimate(
            flops=4 * pairs * nlon * chans * lat_rows,
            bytes_accessed=2 * (grid.size + table.size + pairs * lat_rows * 2 * chans),
            transcendentals=0,
        ),
        name="fourier",
    )(table, jnp.asarray(swap_matrix(TILE, TILE)), grid)
    return out.reshape(count, size, lat_rows, 2 * chans)


def legendre_kernel(tile, parts, block_ref, panel_ref, swap_ref, *rest):
    spectra_refs, far_refs, hold = rest[:parts], rest[parts:-1], rest[-1]
    degrees, latitudes = panel_ref.shape[2:]
    span, size, width = far_refs[0].shape
    block = block_ref[0]
    j = pl.program_id(0)

    def advance(spectra_ref):
        values = spectra_ref[:, 0].reshape(latitudes, width)
        for t in range(degrees // tile):

            @pl.when((t + 1) * tile > block * span)
            def _():
                part = jnp.dot(
                    panel_ref[0, 0, t * tile : (t + 1) * tile, :], values, preferred_element_type=jnp.float32
                )
                hold[j, t * tile : (t + 1) * tile, :] = part.astype(jnp.bfloat16)

    for index, spectra_ref in enumerate(spectra_refs):
        pl.when(j // (size // parts) == index)(functools.partial(advance, spectra_ref))

    @pl.when(j == size - 1)
    def _():
        for k in range(len(far_refs)):
            degree = jnp.bitwise_xor(block, k)

            @pl.when(degree >= block)
            def _():
                for first in range(0, span, TILE):
                    start = pl.multiple_of(degree * span + first, TILE)
                    values = hold[:, pl.ds(start, TILE), :].reshape(size * TILE, width)
                    swapped = jnp.dot(swap_ref[...], values, preferred_element_type=jnp.float32)
                    far_refs[k][first : first + TILE] = swapped.astype(jnp.bfloat16).reshape(TILE, size, width)


def legendre_part(block, legendre, spectra, first):
    count, part_size, lat_rows, width = spectra[0].shape
    parts = len(spectra)
    size = parts * part_size
    _, panels, degrees, latitudes = legendre.shape
    span = degrees // count
    base = panels // 2 + first
    if size % TILE or span % TILE or lat_rows % TILE:
        values = jnp.concatenate(spectra, axis=1).transpose(0, 2, 1, 3).reshape(latitudes, size, width)
        panel = legendre[0, base : base + size]
        result = jnp.einsum("jlt,tjk->ljk", panel, values, preferred_element_type=jnp.float32)
        result = result.astype(jnp.bfloat16).reshape(count, span, size, width)
        return [lax.dynamic_index_in_dim(result, block[0] ^ k, keepdims=False) for k in range(count)]
    tile = min(128, degrees)
    piece = jax.ShapeDtypeStruct((span, size, width), jnp.bfloat16)

    def spectra_spec(part):
        def where(j, b):
            return 0, jnp.clip(j - part * part_size, 0, part_size - 1), 0, 0

        return pl.BlockSpec((count, 1, lat_rows, width), where)

    return pl.pallas_call(
        functools.partial(legendre_kernel, tile, parts),
        out_shape=[piece] * count,
        grid_spec=pltpu.PrefetchScalarGridSpec(
            num_scalar_prefetch=1,
            grid=(size,),
            in_specs=[
                pl.BlockSpec((1, 1, degrees, latitudes), lambda j, b: (0, base + j, 0, 0)),
                pl.BlockSpec((size * TILE, size * TILE), lambda j, b: (0, 0)),
            ]
            + [spectra_spec(part) for part in range(parts)],
            out_specs=[pl.BlockSpec((span, size, width), lambda j, b: (0, 0, 0))] * count,
            scratch_shapes=[pltpu.VMEM((size, degrees, width), jnp.bfloat16)],
        ),
        compiler_params=pltpu.CompilerParams(vmem_limit_bytes=VMEM_LIMIT),
        cost_estimate=pl.CostEstimate(
            flops=2 * size * degrees * latitudes * width,
            bytes_accessed=2 * size * (degrees * latitudes + 2 * degrees * width),
            transcendentals=0,
        ),
        name="legendre",
    )(block, legendre, jnp.asarray(swap_matrix(size, TILE)), *spectra)


def mixing_kernel(index_ref, mixing_ref, *rest):
    out_ref, hold = rest[-2:]
    _, count, size, width = out_ref.shape
    far_refs = rest[:count]
    chans = width // 2
    me = index_ref[0]
    for row in range(out_ref.shape[0]):
        for k in range(count):
            hold[jnp.bitwise_xor(me, k)] = far_refs[k][row]
        values = hold[...].reshape(count * size, width)
        real, imag = values[:, :chans], values[:, chans:]
        real_w, imag_w = mixing_ref[row, 0], mixing_ref[row, 1]
        out_real = jnp.dot(real, real_w, preferred_element_type=jnp.float32) - jnp.dot(
            imag, imag_w, preferred_element_type=jnp.float32
        )
        out_imag = jnp.dot(real, imag_w, preferred_element_type=jnp.float32) + jnp.dot(
            imag, real_w, preferred_element_type=jnp.float32
        )
        out_ref[row, :, :, :chans] = out_real.astype(jnp.bfloat16).reshape(count, size, chans)
        out_ref[row, :, :, chans:] = out_imag.astype(jnp.bfloat16).reshape(count, size, chans)


def mix_part(index, mixing, far, before, chunk, per_dev):
    count = len(far)
    span, size, width = far[0].shape
    chans = width // 2
    if size % TILE:
        stack = jnp.stack([far[k] for k in range(count)])
        stack = jnp.take(stack, jnp.arange(count) ^ index[0], axis=0)
        real_w, imag_w = mixing[:, 0], mixing[:, 1]
        weight = jnp.concatenate(
            [jnp.concatenate([real_w, imag_w], axis=-1), jnp.concatenate([-imag_w, real_w], axis=-1)], axis=1
        )
        mixed = jnp.einsum("bljk,lkn->lbjn", stack, weight, preferred_element_type=jnp.float32)
        return mixed.astype(jnp.bfloat16)
    step = min(2, span)
    operands = [index, mixing, *far]
    specs = [
        pl.BlockSpec((step, 2, chans, chans), lambda l, i: (l, 0, 0, 0)),
    ] + [pl.BlockSpec((step, size, width), lambda l, i: (l, 0, 0))] * count
    aliases = {}
    if before is not None:
        aliases = {len(operands): 0}
        operands.append(before)
        specs.append(pl.BlockSpec(memory_space=pl.ANY))
    return pl.pallas_call(
        mixing_kernel,
        out_shape=jax.ShapeDtypeStruct((span, count, per_dev, width), jnp.bfloat16),
        grid_spec=pltpu.PrefetchScalarGridSpec(
            num_scalar_prefetch=1,
            grid=(span // step,),
            in_specs=specs,
            out_specs=pl.BlockSpec((step, count, size, width), lambda l, i: (l, 0, chunk, 0)),
            scratch_shapes=[pltpu.VMEM((count, size, width), jnp.bfloat16)],
        ),
        input_output_aliases=aliases,
        compiler_params=pltpu.CompilerParams(vmem_limit_bytes=VMEM_LIMIT),
        cost_estimate=pl.CostEstimate(
            flops=2 * span * count * size * width * width,
            bytes_accessed=2 * (mixing.size + 2 * span * count * size * width),
            transcendentals=0,
        ),
        name="mix",
    )(*operands)


def on_device(grid, legendre, mixing):
    count = lax.axis_size("ord")
    half = count // 2
    me = lax.axis_index("ord")
    index = me.astype(jnp.int32).reshape(1)
    block = count - 1 - index
    nlon = grid.shape[1]
    per_dev = legendre.shape[1] // 2
    size = min(CHUNK, per_dev)
    chunks = per_dev // size
    parts = min(PARTS, chunks)
    stages = chunks // parts
    rounds = [r for k in range(half) for r in (k, half + k)]
    tables = [jnp.asarray(fourier_table(nlon, count, per_dev, q * size, size)) for q in range(chunks)]
    sending = [fourier(grid, table, count, size) for table in tables]

    def exchange(values):
        return lax.all_to_all(values, "ord", split_axis=0, concat_axis=0, tiled=True)

    def deliver(far):
        landed = [None] * count
        for k in rounds:
            pairs = [(count - 1 - b, b ^ k) for b in range(count) if b ^ k >= b]
            landed[k] = lax.ppermute(far[k], "ord", pairs)
        return landed

    arrived = [exchange(values) for values in sending]
    out = None
    for stage in range(stages):
        first = stage * parts
        far = legendre_part(block, legendre, arrived[first : first + parts], first * size)
        landed = deliver(far)
        out = mix_part(index, mixing, landed, out, stage, per_dev)
    span, _, _, width = out.shape
    return out.reshape(span, count * per_dev, width)


def solution(mesh):
    return jax.shard_map(
        on_device,
        mesh=mesh,
        in_specs=(
            P(("grp", "ord"), None, None),
            P("ord", None, None, None),
            P("ord", None, None, None),
        ),
        out_specs=P(("grp", "ord"), None, None),
        check_vma=False,
    )
```

time: 921 us -> 773 us (0.84)
  waiting for transfers between devices: 696 us -> 536 us
  Pallas kernels: 0 us -> 137 us
  local copies, waits for them, and re-layouts: 113 us -> 0.1 us
  starting transfers between devices: 26.4 us -> 95.5 us
  matrix products: 68.3 us -> 0 us
  other arithmetic: 13.2 us -> 0 us
    all_to_all x2 -> x4, waiting for transfers between devices: 696 us -> 230 us  [exchange(): lax.all_to_all(values, 'ord', split_axis=0, concat_axis=0, tiled=True)]
    ppermute x0 -> x32, waiting for transfers between devices: none -> 307 us  [deliver(): landed[k] = lax.ppermute(far[k], 'ord', pairs)]
    pallas_call x0 -> x8, Pallas kernels: none -> 137 us  [the longest x4 55.4 us: fourier(): pl.pallas_call(functools.partial(fourier_kernel, rows_step), out_shape=ja...]
    dot_general x4 -> x0, matrix products: 68.3 us -> none  [the longest x1 25.9 us: on_device(): jnp.einsum('tnc,nk->tkc', grid, table, preferred_element_type=jnp.float32)]
    ppermute x0 -> x32, starting transfers between devices: none -> 68.1 us  [deliver(): landed[k] = lax.ppermute(far[k], 'ord', pairs)]
    reshape x2 -> x0, local copies, waits for them, and re-layouts: 43 us -> none  [on_device(): sending = spectra.reshape(lat_rows, orders, 2 * chans)]
    all_to_all x2 -> x0, local copies, waits for them, and re-layouts: 28.5 us -> none  [the longest x1 14.4 us: on_device(): lax.all_to_all(coeffs, 'ord', split_axis=1, concat_axis=0, tiled=True)]
    slice x1 -> x0, local copies, waits for them, and re-layouts: 13.7 us -> none  [on_device(): coeffs = legendre_tiles(panels[:per_dev], arrived, first)]
  transfers between devices with their start and end apart: 2 -> 36, of which waited for: 2 -> 17; matrix products, arithmetic and copies ran while one was open for 3% -> 0% of each run, Pallas kernels for 0% -> 14%
where the time goes in v1:
time: 773 us; the launch traced here: 770 us
  waiting for transfers between devices  536 us (69%)
  Pallas kernels  137 us (18%)
  starting transfers between devices  95.5 us (12%)
    ppermute x32, waiting for transfers between devices, deliver(): landed[k] = lax.ppermute(far[k], 'ord', pairs)  307 us
    all_to_all x4, waiting for transfers between devices, exchange(): lax.all_to_all(values, 'ord', split_axis=0, concat_axis=0, tiled=True)  230 us
    ppermute x32, starting transfers between devices, deliver(): landed[k] = lax.ppermute(far[k], 'ord', pairs)  68.1 us
    pallas_call x4, Pallas kernels, fourier(): pl.pallas_call(functools.partial(fourier_kernel, rows_step), out_shape=ja...  55.4 us
    pallas_call x2, Pallas kernels, legendre_part(): pl.pallas_call(functools.partial(legendre_kernel, tile, parts), out_shape...  48.8 us
    pallas_call x2, Pallas kernels, mix_part(): pl.pallas_call(mixing_kernel, out_shape=jax.ShapeDtypeStruct((span, count...  33 us
    all_to_all x4, starting transfers between devices, exchange(): lax.all_to_all(values, 'ord', split_axis=0, concat_axis=0, tiled=True)  27.5 us
  transfers between devices with their start and end apart: 36, of which 17 were waited for; matrix products, arithmetic and copies ran while one was open for 0% of the time, Pallas kernels for 14%

profile of v1, /device:TPU:21, one launch (start us, length us, event | category | flops | bytes accessed | tf_op | source)
XLA Modules:
  0.0 769.7 jit_solution(2308254416744537640)
XLA Ops:
  0.0 13.8 %fourier.6 = bf16[128,32,512]{2,1,0:T(8,128)(2,1)} custom-call(bf16[256,1024]{1,0:T(8,128)(2,1)} %constant.16.clone.table_ref, bf16[256,256]{1,0:T(8,128)(2,1)} %constant.20.clone.swap_ref, bf16[32,1024,256]{2,1,0:T(8,128)(2,1)} %grid_ref.7), custom_call_target="tpu_custom_call" | custom-call | flops 4294967296 | bytes 21495808 | tf_op jit(solution)/shard_map/fourier/pallas_call | solution.py:63
  13.8 6.4 all-to-all-start.2
  20.3 13.9 %fourier.7 = bf16[128,32,512]{2,1,0:T(8,128)(2,1)} custom-call(bf16[256,1024]{1,0:T(8,128)(2,1)} %constant.17.clone.table_ref, bf16[256,256]{1,0:T(8,128)(2,1)} %constant.20.clone.swap_ref, bf16[32,1024,256]{2,1,0:T(8,128)(2,1)} %grid_ref.7), custom_call_target="tpu_custom_call" | custom-call | flops 4294967296 | bytes 21495808 | tf_op jit(solution)/shard_map/fourier/pallas_call | solution.py:63
  34.1 76.5 %all-to-all-done.2.rest_0_ = bf16[16,8,32,512]{3,2,1,0:T(8,128)(2,1)} async-done(((bf16[16,8,32,512]{3,2,1,0:T(8,128)(2,1)}), bf16[16,8,32,512]{3,2,1,0:T(8,128)(2,1)}, u32[]{:S(2)}, u32[]{:S(2)}) %all-to-all-start.2) | async-done | bytes 4194336 | tf_op jit(solution)/shard_map/all_to_all | solution.py:249
  110.6 7.0 all-to-all-start.3
  117.6 13.8 %fourier.4 = bf16[128,32,512]{2,1,0:T(8,128)(2,1)} custom-call(bf16[256,1024]{1,0:T(8,128)(2,1)} %constant.18.clone.table_ref, bf16[256,256]{1,0:T(8,128)(2,1)} %constant.20.clone.swap_ref, bf16[32,1024,256]{2,1,0:T(8,128)(2,1)} %grid_ref.7), custom_call_target="tpu_custom_call" | custom-call | flops 4294967296 | bytes 21495808 | tf_op jit(solution)/shard_map/fourier/pallas_call | solution.py:63
  131.5 76.5 %all-to-all-done.3.rest_1_ = bf16[16,8,32,512]{3,2,1,0:T(8,128)(2,1)} async-done(((bf16[16,8,32,512]{3,2,1,0:T(8,128)(2,1)}), bf16[16,8,32,512]{3,2,1,0:T(8,128)(2,1)}, u32[]{:S(2)}, u32[]{:S(2)}) %all-to-all-start.3) | async-done | bytes 4194336 | tf_op jit(solution)/shard_map/all_to_all | solution.py:249
  208.0 7.0 all-to-all-start
  215.0 13.9 %fourier.5 = bf16[128,32,512]{2,1,0:T(8,128)(2,1)} custom-call(bf16[256,1024]{1,0:T(8,128)(2,1)} %constant.19.clone.table_ref, bf16[256,256]{1,0:T(8,128)(2,1)} %constant.20.clone.swap_ref, bf16[32,1024,256]{2,1,0:T(8,128)(2,1)} %grid_ref.7), custom_call_target="tpu_custom_call" | custom-call | flops 4294967296 | bytes 21495808 | tf_op jit(solution)/shard_map/fourier/pallas_call | solution.py:63
  228.9 76.5 %all-to-all-done.rest_0_ = bf16[16,8,32,512]{3,2,1,0:T(8,128)(2,1)} async-done(((bf16[16,8,32,512]{3,2,1,0:T(8,128)(2,1)}), bf16[16,8,32,512]{3,2,1,0:T(8,128)(2,1)}, u32[]{:S(2)}, u32[]{:S(2)}) %all-to-all-start) | async-done | bytes 4194336 | tf_op jit(solution)/shard_map/all_to_all | solution.py:249
  305.4 7.0 all-to-all-start.1
  312.4 24.3 %legendre.3 = (bf16[32,16,512]{2,1,0:T(8,128)(2,1)}, bf16[32,16,512]{2,1,0:T(8,128)(2,1)}, bf16[32,16,512]{2,1,0:T(8,128)(2,1)}, bf16[32,16,512]{2,1,0:T(8,128)(...) custom-call(s32[1]{0:T(128)S(6)} %sub.3.block_ref, ...), custom_call_target="tpu_custom_call" | custom-call | flops 4294967296 | bytes 25165824 | tf_op jit(solution)/shard_map/legendre/pallas_call | solution.py:142
  336.7 4.2 collective-permute-start.17
  340.9 1.9 collective-permute-start.18
  342.9 1.9 collective-permute-start.19
  345.5 119.0 %collective-permute-done.16.rest_0_ = bf16[32,16,512]{2,1,0:T(8,128)(2,1)S(1)} collective-permute-done((bf16[32,16,512]{2,1,0:T(8,128)(2,1)}, bf16[32,16,512]{2,1,0:T(8,128)(2,1)S(1)}, u32[]{:S(2)}, u32[]{:S(2)}) %collective-permute-start.16) | collective-permute-done | bytes 524320 | tf_op jit(solution)/shard_map/ppermute | solution.py:255
  465.2 33.0 %collective-permute-done.17.rest_1_ = bf16[32,16,512]{2,1,0:T(8,128)(2,1)S(1)} collective-permute-done((bf16[32,16,512]{2,1,0:T(8,128)(2,1)}, bf16[32,16,512]{2,1,0:T(8,128)(2,1)S(1)}, u32[]{:S(2)}, u32[]{:S(2)}) %collective-permute-start.17) | collective-permute-done | bytes 524320 | tf_op jit(solution)/shard_map/ppermute | solution.py:255
  499.7 15.4 %collective-permute-done.18.rest_2_ = bf16[32,16,512]{2,1,0:T(8,128)(2,1)S(1)} collective-permute-done((bf16[32,16,512]{2,1,0:T(8,128)(2,1)}, bf16[32,16,512]{2,1,0:T(8,128)(2,1)S(1)}, u32[]{:S(2)}, u32[]{:S(2)}) %collective-permute-start.18) | collective-permute-done | bytes 524320 | tf_op jit(solution)/shard_map/ppermute | solution.py:255
  516.5 4.7 collective-permute-done.19.rest_3_
  521.2 1.9 collective-permute-start.24
  523.1 1.9 collective-permute-start.25
  525.1 1.9 collective-permute-start.26
  527.0 6.4 collective-permute-start.27
  533.5 24.5 %legendre.2 = (bf16[32,16,512]{2,1,0:T(8,128)(2,1)}, bf16[32,16,512]{2,1,0:T(8,128)(2,1)}, bf16[32,16,512]{2,1,0:T(8,128)(2,1)}, bf16[32,16,512]{2,1,0:T(8,128)(...) custom-call(s32[1]{0:T(128)S(6)} %sub.3.block_ref, ...), custom_call_target="tpu_custom_call" | custom-call | flops 4294967296 | bytes 25165824 | tf_op jit(solution)/shard_map/legendre/pallas_call | solution.py:142
  558.1 1.9 collective-permute-start.28
  560.0 1.9 collective-permute-start.29
  562.0 4.0 collective-permute-start.30
  566.7 5.0 collective-permute-done.27.rest_11_
  571.7 3.3 collective-permute-done.28.rest_12_
  575.0 1.9 collective-permute-start.1
  576.9 17.0 %collective-permute-done.29.rest_13_ = bf16[32,16,512]{2,1,0:T(8,128)(2,1)S(1)} collective-permute-done((bf16[32,16,512]{2,1,0:T(8,128)(2,1)S(1)}, bf16[32,16,512]{2,1,0:T(8,128)(2,1)S(1)}, u32[]{:S(2)}, u32[]{:S(2)}) %collective-permute-start.29) | collective-permute-done | bytes 524320 | tf_op jit(solution)/shard_map/ppermute | solution.py:255
  595.9 1.9 collective-permute-start.3
  598.5 5.3 collective-permute-done.rest_0_
  604.5 63.1 %collective-permute-done.1.rest_1_ = bf16[32,16,512]{2,1,0:T(8,128)(2,1)S(1)} collective-permute-done((bf16[32,16,512]{2,1,0:T(8,128)(2,1)}, bf16[32,16,512]{2,1,0:T(8,128)(2,1)S(1)}, u32[]{:S(2)}, u32[]{:S(2)}) %collective-permute-start.1) | collective-permute-done | bytes 524320 | tf_op jit(solution)/shard_map/ppermute | solution.py:255
  668.3 16.2 %collective-permute-done.2.rest_2_ = bf16[32,16,512]{2,1,0:T(8,128)(2,1)S(1)} collective-permute-done((bf16[32,16,512]{2,1,0:T(8,128)(2,1)}, bf16[32,16,512]{2,1,0:T(8,128)(2,1)S(1)}, u32[]{:S(2)}, u32[]{:S(2)}) %collective-permute-start.2) | collective-permute-done | bytes 524320 | tf_op jit(solution)/shard_map/ppermute | solution.py:255
  685.2 5.3 collective-permute-done.3.rest_3_
  692.4 1.9 collective-permute-start.9
  694.4 1.9 collective-permute-start.10
  696.3 6.3 collective-permute-start.11
  702.6 1.9 collective-permute-start.12
  704.5 3.3 collective-permute-done.8.rest_8_
  707.9 3.4 collective-permute-start.13
  711.3 6.6 collective-permute-done.9.rest_9_
  717.9 3.7 collective-permute-start.14
  721.6 9.4 %collective-permute-done.10.rest_10_ = bf16[32,16,512]{2,1,0:T(8,128)(2,1)S(1)} collective-permute-done((bf16[32,16,512]{2,1,0:T(8,128)(2,1)}, bf16[32,16,512]{2,1,0:T(8,128)(2,1)S(1)}, u32[]{:S(2)}, u32[]{:S(2)}) %collective-permute-start.10) | collective-permute-done | bytes 524320 | tf_op jit(solution)/shard_map/ppermute | solution.py:255
  731.0 5.4 collective-permute-start.15
  736.4 16.5 %mix.2.rest_16_ = bf16[32,16,32,512]{3,2,1,0:T(8,128)(2,1)} custom-call(s32[1]{0:T(128)} %bitcast.index_ref, bf16[32,2,256,256]{3,2,1,0:T(8,128)(2,1)} %mixing_ref.3, bf16[32,16,512]{2,1,0:T(8,128)(2,1)} %copy-done, bf16[32,16,512]{2,1,0:T(8,128)(2,1)} %copy-done.1, bf16[32,16,512]{2,1,0:T(8,128)(2,1)} %copy-done.2, bf16[32,16,512]{2,1,0:T(8,128)(2,1)} %copy-done.3, ...), custom_call_target="tpu_custom_call" | custom-call | flops 4294967296 | bytes 25165824 | tf_op jit(solution)/shard_map/mix/pallas_call | solution.py:211
  753.1 16.5 %mix.3 = bf16[32,16,32,512]{3,2,1,0:T(8,128)(2,1)} custom-call(s32[1]{0:T(128)} %bitcast.index_ref, bf16[32,2,256,256]{3,2,1,0:T(8,128)(2,1)} %mixing_ref.3, bf16[32,16,512]{2,1,0:T(8,128)(2,1)} %copy-done.8, bf16[32,16,512]{2,1,0:T(8,128)(2,1)} %copy-done.10, bf16[32,16,512]{2,1,0:T(8,128)(2,1)} %copy-done.11, ...), custom_call_target="tpu_custom_call", output_to_operand_aliasing={{}: (18, {})} | custom-call | flops 4294967296 | bytes 25165824 | tf_op jit(solution)/shard_map/mix/pallas_call | solution.py:211
  (82 shorter events, 11.7 us)
Async XLA Ops:
  13.8 96.8 %all-to-all-start.2 = ((bf16[16,8,32,512]{3,2,1,0:T(8,128)(2,1)}), bf16[16,8,32,512]{3,2,1,0:T(8,128)(2,1)}, u32[]{:S(2)}, u32[]{:S(2)}) async-start(bf16[16,8,32,512]{3,2,1,0:T(8,128)(2,1)} %bitcast.9), calls=%async_computation.2 | async-start | bytes 8388608 | tf_op jit(solution)/shard_map/all_to_all | solution.py:249
  110.6 97.4 %all-to-all-start.3 = ((bf16[16,8,32,512]{3,2,1,0:T(8,128)(2,1)}), bf16[16,8,32,512]{3,2,1,0:T(8,128)(2,1)}, u32[]{:S(2)}, u32[]{:S(2)}) async-start(bf16[16,8,32,512]{3,2,1,0:T(8,128)(2,1)} %bitcast.7), calls=%async_computation.3 | async-start | bytes 8388608 | tf_op jit(solution)/shard_map/all_to_all | solution.py:249
  208.0 97.4 %all-to-all-start = ((bf16[16,8,32,512]{3,2,1,0:T(8,128)(2,1)}), bf16[16,8,32,512]{3,2,1,0:T(8,128)(2,1)}, u32[]{:S(2)}, u32[]{:S(2)}) async-start(bf16[16,8,32,512]{3,2,1,0:T(8,128)(2,1)} %bitcast.8), calls=%async_computation | async-start | bytes 8388608 | tf_op jit(solution)/shard_map/all_to_all | solution.py:249
  305.4 228.1 %all-to-all-start.1 = ((bf16[16,8,32,512]{3,2,1,0:T(8,128)(2,1)}), bf16[16,8,32,512]{3,2,1,0:T(8,128)(2,1)}, u32[]{:S(2)}, u32[]{:S(2)}) async-start(bf16[16,8,32,512]{3,2,1,0:T(8,128)(2,1)} %bitcast.6), calls=%async_computation.1 | async-start | bytes 8388608 | tf_op jit(solution)/shard_map/all_to_all | solution.py:249
  336.7 127.9 %collective-permute-start.16 = (bf16[32,16,512]{2,1,0:T(8,128)(2,1)}, bf16[32,16,512]{2,1,0:T(8,128)(2,1)S(1)}, u32[]{:S(2)}, u32[]{:S(2)}) collective-permute-start(bf16[32,16,512]{2,1,0:T(8,128)(2,1)} %get-tuple-element.53), channel_id=1, source_target_pairs={{15,0},{14,1},{13,2},{12,3},{11,4},{10,5},{9,6},{8,7},{7,8},{6,9},... | collective-permute-start | bytes 1572872 | tf_op jit(solution)/shard_map/ppermute | solution.py:255
  336.7 161.5 %collective-permute-start.17 = (bf16[32,16,512]{2,1,0:T(8,128)(2,1)}, bf16[32,16,512]{2,1,0:T(8,128)(2,1)S(1)}, u32[]{:S(2)}, u32[]{:S(2)}) collective-permute-start(bf16[32,16,512]{2,1,0:T(8,128)(2,1)} %get-tuple-element.54), channel_id=1, source_target_pairs={{15,1},{13,3},{11,5},{9,7},{7,9},{5,11},{3,13},{1,15},{31,17},{29,... | collective-permute-start | bytes 1572872 | tf_op jit(solution)/shard_map/ppermute | solution.py:255
  340.9 174.2 %collective-permute-start.18 = (bf16[32,16,512]{2,1,0:T(8,128)(2,1)}, bf16[32,16,512]{2,1,0:T(8,128)(2,1)S(1)}, u32[]{:S(2)}, u32[]{:S(2)}) collective-permute-start(bf16[32,16,512]{2,1,0:T(8,128)(2,1)} %get-tuple-element.55), channel_id=1, source_target_pairs={{15,2},{14,3},{11,6},{10,7},{7,10},{6,11},{3,14},{2,15},{31,18},{3... | collective-permute-start | bytes 1572872 | tf_op jit(solution)/shard_map/ppermute | solution.py:255
  342.9 178.3 %collective-permute-start.19 = (bf16[32,16,512]{2,1,0:T(8,128)(2,1)}, bf16[32,16,512]{2,1,0:T(8,128)(2,1)S(1)}, u32[]{:S(2)}, u32[]{:S(2)}) collective-permute-start(bf16[32,16,512]{2,1,0:T(8,128)(2,1)} %get-tuple-element.56), channel_id=1, source_target_pairs={{15,3},{14,2},{11,7},{10,6},{7,11},{6,10},{3,15},{2,14},{31,19},{3... | collective-permute-start | bytes 1572872 | tf_op jit(solution)/shard_map/ppermute | solution.py:255
  344.8 178.3 %collective-permute-start.20 = (bf16[32,16,512]{2,1,0:T(8,128)(2,1)}, bf16[32,16,512]{2,1,0:T(8,128)(2,1)S(1)}, u32[]{:S(2)}, u32[]{:S(2)}) collective-permute-start(bf16[32,16,512]{2,1,0:T(8,128)(2,1)} %get-tuple-element.57), channel_id=1, source_target_pairs={{15,4},{14,5},{13,6},{12,7},{7,12},{6,13},{5,14},{4,15},{31,20},{3... | collective-permute-start | bytes 1572872 | tf_op jit(solution)/shard_map/ppermute | solution.py:255
  464.5 93.4 %copy-start = (bf16[32,16,512]{2,1,0:T(8,128)(2,1)}, bf16[32,16,512]{2,1,0:T(8,128)(2,1)S(1)}, u32[]{:S(2)}) copy-start(bf16[32,16,512]{2,1,0:T(8,128)(2,1)S(1)} %collective-permute-done.16.rest_0_) | copy-start | bytes 1572868
  464.5 60.5 %collective-permute-start.21 = (bf16[32,16,512]{2,1,0:T(8,128)(2,1)}, bf16[32,16,512]{2,1,0:T(8,128)(2,1)S(1)}, u32[]{:S(2)}, u32[]{:S(2)}) collective-permute-start(bf16[32,16,512]{2,1,0:T(8,128)(2,1)} %get-tuple-element.58), channel_id=1, source_target_pairs={{15,5},{14,4},{13,7},{12,6},{7,13},{6,12},{5,15},{4,14},{31,21},{3... | collective-permute-start | bytes 1572872 | tf_op jit(solution)/shard_map/ppermute | solution.py:255
  498.2 59.7 %copy-start.1 = (bf16[32,16,512]{2,1,0:T(8,128)(2,1)}, bf16[32,16,512]{2,1,0:T(8,128)(2,1)S(1)}, u32[]{:S(2)}) copy-start(bf16[32,16,512]{2,1,0:T(8,128)(2,1)S(1)} %collective-permute-done.17.rest_1_) | copy-start | bytes 1572868
  498.2 28.8 %collective-permute-start.22 = (bf16[32,16,512]{2,1,0:T(8,128)(2,1)}, bf16[32,16,512]{2,1,0:T(8,128)(2,1)}, u32[]{:S(2)}, u32[]{:S(2)}) collective-permute-start(bf16[32,16,512]{2,1,0:T(8,128)(2,1)} %get-tuple-element.59), channel_id=1, source_target_pairs={{15,6},{14,7},{13,4},{12,5},{7,14},{6,15},{5,12},{4,13},{31,22},{3... | collective-permute-start | bytes 1572872 | tf_op jit(solution)/shard_map/ppermute | solution.py:255
  515.1 42.9 %collective-permute-start.23 = (bf16[32,16,512]{2,1,0:T(8,128)(2,1)}, bf16[32,16,512]{2,1,0:T(8,128)(2,1)}, u32[]{:S(2)}, u32[]{:S(2)}) collective-permute-start(bf16[32,16,512]{2,1,0:T(8,128)(2,1)} %get-tuple-element.60), channel_id=1, source_target_pairs={{15,7},{14,6},{13,5},{12,4},{7,15},{6,14},{5,13},{4,12},{31,23},{3... | collective-permute-start | bytes 1572872 | tf_op jit(solution)/shard_map/ppermute | solution.py:255
  521.2 38.8 %collective-permute-start.24 = (bf16[32,16,512]{2,1,0:T(8,128)(2,1)}, bf16[32,16,512]{2,1,0:T(8,128)(2,1)}, u32[]{:S(2)}, u32[]{:S(2)}) collective-permute-start(bf16[32,16,512]{2,1,0:T(8,128)(2,1)} %get-tuple-element.61), channel_id=1, source_target_pairs={{15,8},{14,9},{13,10},{12,11},{11,12},{10,13},{9,14},{8,15},{31,24... | collective-permute-start | bytes 1572872 | tf_op jit(solution)/shard_map/ppermute | solution.py:255
  523.1 38.8 %collective-permute-start.25 = (bf16[32,16,512]{2,1,0:T(8,128)(2,1)}, bf16[32,16,512]{2,1,0:T(8,128)(2,1)}, u32[]{:S(2)}, u32[]{:S(2)}) collective-permute-start(bf16[32,16,512]{2,1,0:T(8,128)(2,1)} %get-tuple-element.62), channel_id=1, source_target_pairs={{15,9},{14,8},{13,11},{12,10},{11,13},{10,12},{9,15},{8,14},{31,25... | collective-permute-start | bytes 1572872 | tf_op jit(solution)/shard_map/ppermute | solution.py:255
  525.1 40.9 %collective-permute-start.26 = (bf16[32,16,512]{2,1,0:T(8,128)(2,1)}, bf16[32,16,512]{2,1,0:T(8,128)(2,1)}, u32[]{:S(2)}, u32[]{:S(2)}) collective-permute-start(bf16[32,16,512]{2,1,0:T(8,128)(2,1)} %get-tuple-element.63), channel_id=1, source_target_pairs={{15,10},{14,11},{13,8},{12,9},{11,14},{10,15},{9,12},{8,13},{31,26... | collective-permute-start | bytes 1572872 | tf_op jit(solution)/shard_map/ppermute | solution.py:255
  527.0 44.6 %collective-permute-start.27 = (bf16[32,16,512]{2,1,0:T(8,128)(2,1)}, bf16[32,16,512]{2,1,0:T(8,128)(2,1)}, u32[]{:S(2)}, u32[]{:S(2)}) collective-permute-start(bf16[32,16,512]{2,1,0:T(8,128)(2,1)} %get-tuple-element.64), channel_id=1, source_target_pairs={{15,11},{14,10},{13,9},{12,8},{11,15},{10,14},{9,13},{8,12},{31,27... | collective-permute-start | bytes 1572872 | tf_op jit(solution)/shard_map/ppermute | solution.py:255
  558.1 16.9 %collective-permute-start.28 = (bf16[32,16,512]{2,1,0:T(8,128)(2,1)S(1)}, bf16[32,16,512]{2,1,0:T(8,128)(2,1)S(1)}, u32[]{:S(2)}, u32[]{:S(2)}) collective-permute-start(bf16[32,16,512]{2,1,0:T(8,128)(2,1)S(1)} %copy-done.24), channel_id=1, source_target_pairs={{15,12},{14,13},{13,14},{12,15},{11,8},{10,9},{9,10},{8,11},{31,28... | collective-permute-start | bytes 1572872 | tf_op jit(solution)/shard_map/ppermute | solution.py:255
  560.0 33.9 %collective-permute-start.29 = (bf16[32,16,512]{2,1,0:T(8,128)(2,1)S(1)}, bf16[32,16,512]{2,1,0:T(8,128)(2,1)S(1)}, u32[]{:S(2)}, u32[]{:S(2)}) collective-permute-start(bf16[32,16,512]{2,1,0:T(8,128)(2,1)S(1)} %copy-done.23), channel_id=1, source_target_pairs={{15,13},{14,12},{13,15},{12,14},{11,9},{10,8},{9,11},{8,10},{31,29... | collective-permute-start | bytes 1572872 | tf_op jit(solution)/shard_map/ppermute | solution.py:255
  562.0 33.9 %collective-permute-start.30 = (bf16[32,16,512]{2,1,0:T(8,128)(2,1)S(1)}, bf16[32,16,512]{2,1,0:T(8,128)(2,1)S(1)}, u32[]{:S(2)}, u32[]{:S(2)}) collective-permute-start(bf16[32,16,512]{2,1,0:T(8,128)(2,1)S(1)} %copy-done.22), channel_id=1, source_target_pairs={{15,14},{14,15},{13,12},{12,13},{11,10},{10,11},{9,8},{8,9},{31,30... | collective-permute-start | bytes 1572872 | tf_op jit(solution)/shard_map/ppermute | solution.py:255
  566.0 31.8 %collective-permute-start.31 = (bf16[32,16,512]{2,1,0:T(8,128)(2,1)S(1)}, bf16[32,16,512]{2,1,0:T(8,128)(2,1)S(1)}, u32[]{:S(2)}, u32[]{:S(2)}) collective-permute-start(bf16[32,16,512]{2,1,0:T(8,128)(2,1)S(1)} %copy-done.21), channel_id=1, source_target_pairs={{15,15},{14,14},{13,13},{12,12},{11,11},{10,10},{9,9},{8,8},{31,31... | collective-permute-start | bytes 1572872 | tf_op jit(solution)/shard_map/ppermute | solution.py:255
  571.7 32.1 %collective-permute-start = (bf16[32,16,512]{2,1,0:T(8,128)(2,1)}, bf16[32,16,512]{2,1,0:T(8,128)(2,1)S(1)}, u32[]{:S(2)}, u32[]{:S(2)}) collective-permute-start(bf16[32,16,512]{2,1,0:T(8,128)(2,1)} %get-tuple-element.37), channel_id=1, source_target_pairs={{15,0},{14,1},{13,2},{12,3},{11,4},{10,5},{9,6},{8,7},{7,8},{6,9},... | collective-permute-start | bytes 1572872 | tf_op jit(solution)/shard_map/ppermute | solution.py:255
  575.0 161.4 %copy-start.6 = (bf16[32,16,512]{2,1,0:T(8,128)(2,1)}, bf16[32,16,512]{2,1,0:T(8,128)(2,1)S(1)}, u32[]{:S(2)}) copy-start(bf16[32,16,512]{2,1,0:T(8,128)(2,1)S(1)} %collective-permute-done.28.rest_12_) | copy-start | bytes 1572868
  575.0 92.6 %collective-permute-start.1 = (bf16[32,16,512]{2,1,0:T(8,128)(2,1)}, bf16[32,16,512]{2,1,0:T(8,128)(2,1)S(1)}, u32[]{:S(2)}, u32[]{:S(2)}) collective-permute-start(bf16[32,16,512]{2,1,0:T(8,128)(2,1)} %get-tuple-element.38), channel_id=1, source_target_pairs={{15,1},{13,3},{11,5},{9,7},{7,9},{5,11},{3,13},{1,15},{31,17},{29,... | collective-permute-start | bytes 1572872 | tf_op jit(solution)/shard_map/ppermute | solution.py:255
  593.9 142.4 %copy-start.7 = (bf16[32,16,512]{2,1,0:T(8,128)(2,1)}, bf16[32,16,512]{2,1,0:T(8,128)(2,1)S(1)}, u32[]{:S(2)}) copy-start(bf16[32,16,512]{2,1,0:T(8,128)(2,1)S(1)} %collective-permute-done.29.rest_13_) | copy-start | bytes 1572868
  593.9 90.5 %collective-permute-start.2 = (bf16[32,16,512]{2,1,0:T(8,128)(2,1)}, bf16[32,16,512]{2,1,0:T(8,128)(2,1)S(1)}, u32[]{:S(2)}, u32[]{:S(2)}) collective-permute-start(bf16[32,16,512]{2,1,0:T(8,128)(2,1)} %get-tuple-element.39), channel_id=1, source_target_pairs={{15,2},{14,3},{11,6},{10,7},{7,10},{6,11},{3,14},{2,15},{31,18},{3... | collective-permute-start | bytes 1572872 | tf_op jit(solution)/shard_map/ppermute | solution.py:255
  595.9 140.5 %copy-start.9 = (bf16[32,16,512]{2,1,0:T(8,128)(2,1)}, bf16[32,16,512]{2,1,0:T(8,128)(2,1)S(1)}, u32[]{:S(2)}) copy-start(bf16[32,16,512]{2,1,0:T(8,128)(2,1)S(1)} %collective-permute-done.30.rest_14_) | copy-start | bytes 1572868
  595.9 94.6 %collective-permute-start.3 = (bf16[32,16,512]{2,1,0:T(8,128)(2,1)}, bf16[32,16,512]{2,1,0:T(8,128)(2,1)S(1)}, u32[]{:S(2)}, u32[]{:S(2)}) collective-permute-start(bf16[32,16,512]{2,1,0:T(8,128)(2,1)} %get-tuple-element.40), channel_id=1, source_target_pairs={{15,3},{14,2},{11,7},{10,6},{7,11},{6,10},{3,15},{2,14},{31,19},{3... | collective-permute-start | bytes 1572872 | tf_op jit(solution)/shard_map/ppermute | solution.py:255
  597.8 138.6 %copy-start.12 = (bf16[32,16,512]{2,1,0:T(8,128)(2,1)}, bf16[32,16,512]{2,1,0:T(8,128)(2,1)S(1)}, u32[]{:S(2)}) copy-start(bf16[32,16,512]{2,1,0:T(8,128)(2,1)S(1)} %collective-permute-done.31.rest_15_) | copy-start | bytes 1572868
  597.8 94.6 %collective-permute-start.4 = (bf16[32,16,512]{2,1,0:T(8,128)(2,1)}, bf16[32,16,512]{2,1,0:T(8,128)(2,1)S(1)}, u32[]{:S(2)}, u32[]{:S(2)}) collective-permute-start(bf16[32,16,512]{2,1,0:T(8,128)(2,1)} %get-tuple-element.41), channel_id=1, source_target_pairs={{15,4},{14,5},{13,6},{12,7},{7,12},{6,13},{5,14},{4,15},{31,20},{3... | collective-permute-start | bytes 1572872 | tf_op jit(solution)/shard_map/ppermute | solution.py:255
  603.8 149.1 %copy-start.8 = (bf16[32,16,512]{2,1,0:T(8,128)(2,1)}, bf16[32,16,512]{2,1,0:T(8,128)(2,1)S(1)}, u32[]{:S(2)}) copy-start(bf16[32,16,512]{2,1,0:T(8,128)(2,1)S(1)} %collective-permute-done.rest_0_) | copy-start | bytes 1572868
  603.8 90.5 %collective-permute-start.5 = (bf16[32,16,512]{2,1,0:T(8,128)(2,1)}, bf16[32,16,512]{2,1,0:T(8,128)(2,1)S(1)}, u32[]{:S(2)}, u32[]{:S(2)}) collective-permute-start(bf16[32,16,512]{2,1,0:T(8,128)(2,1)} %get-tuple-element.42), channel_id=1, source_target_pairs={{15,5},{14,4},{13,7},{12,6},{7,13},{6,12},{5,15},{4,14},{31,21},{3... | collective-permute-start | bytes 1572872 | tf_op jit(solution)/shard_map/ppermute | solution.py:255
  667.6 85.3 %copy-start.10 = (bf16[32,16,512]{2,1,0:T(8,128)(2,1)}, bf16[32,16,512]{2,1,0:T(8,128)(2,1)S(1)}, u32[]{:S(2)}) copy-start(bf16[32,16,512]{2,1,0:T(8,128)(2,1)S(1)} %collective-permute-done.1.rest_1_) | copy-start | bytes 1572868
  667.6 28.7 %collective-permute-start.6 = (bf16[32,16,512]{2,1,0:T(8,128)(2,1)}, bf16[32,16,512]{2,1,0:T(8,128)(2,1)S(1)}, u32[]{:S(2)}, u32[]{:S(2)}) collective-permute-start(bf16[32,16,512]{2,1,0:T(8,128)(2,1)} %get-tuple-element.43), channel_id=1, source_target_pairs={{15,6},{14,7},{13,4},{12,5},{7,14},{6,15},{5,12},{4,13},{31,22},{3... | collective-permute-start | bytes 1572872 | tf_op jit(solution)/shard_map/ppermute | solution.py:255
  684.5 68.5 %copy-start.11 = (bf16[32,16,512]{2,1,0:T(8,128)(2,1)}, bf16[32,16,512]{2,1,0:T(8,128)(2,1)S(1)}, u32[]{:S(2)}) copy-start(bf16[32,16,512]{2,1,0:T(8,128)(2,1)S(1)} %collective-permute-done.2.rest_2_) | copy-start | bytes 1572868
  684.5 18.1 %collective-permute-start.7 = (bf16[32,16,512]{2,1,0:T(8,128)(2,1)}, bf16[32,16,512]{2,1,0:T(8,128)(2,1)S(1)}, u32[]{:S(2)}, u32[]{:S(2)}) collective-permute-start(bf16[32,16,512]{2,1,0:T(8,128)(2,1)} %get-tuple-element.44), channel_id=1, source_target_pairs={{15,7},{14,6},{13,5},{12,4},{7,15},{6,14},{5,13},{4,12},{31,23},{3... | collective-permute-start | bytes 1572872 | tf_op jit(solution)/shard_map/ppermute | solution.py:255
  690.5 62.5 %copy-start.13 = (bf16[32,16,512]{2,1,0:T(8,128)(2,1)}, bf16[32,16,512]{2,1,0:T(8,128)(2,1)S(1)}, u32[]{:S(2)}) copy-start(bf16[32,16,512]{2,1,0:T(8,128)(2,1)S(1)} %collective-permute-done.3.rest_3_) | copy-start | bytes 1572868
  690.5 17.4 %collective-permute-start.8 = (bf16[32,16,512]{2,1,0:T(8,128)(2,1)}, bf16[32,16,512]{2,1,0:T(8,128)(2,1)S(1)}, u32[]{:S(2)}, u32[]{:S(2)}) collective-permute-start(bf16[32,16,512]{2,1,0:T(8,128)(2,1)} %get-tuple-element.45), channel_id=1, source_target_pairs={{15,8},{14,9},{13,10},{12,11},{11,12},{10,13},{9,14},{8,15},{31,24... | collective-permute-start | bytes 1572872 | tf_op jit(solution)/shard_map/ppermute | solution.py:255
  692.4 60.5 %copy-start.14 = (bf16[32,16,512]{2,1,0:T(8,128)(2,1)}, bf16[32,16,512]{2,1,0:T(8,128)(2,1)S(1)}, u32[]{:S(2)}) copy-start(bf16[32,16,512]{2,1,0:T(8,128)(2,1)S(1)} %collective-permute-done.4.rest_4_) | copy-start | bytes 1572868
  692.4 25.5 %collective-permute-start.9 = (bf16[32,16,512]{2,1,0:T(8,128)(2,1)}, bf16[32,16,512]{2,1,0:T(8,128)(2,1)S(1)}, u32[]{:S(2)}, u32[]{:S(2)}) collective-permute-start(bf16[32,16,512]{2,1,0:T(8,128)(2,1)} %get-tuple-element.46), channel_id=1, source_target_pairs={{15,9},{14,8},{13,11},{12,10},{11,13},{10,12},{9,15},{8,14},{31,25... | collective-permute-start | bytes 1572872 | tf_op jit(solution)/shard_map/ppermute | solution.py:255
  694.3 58.6 %copy-start.15 = (bf16[32,16,512]{2,1,0:T(8,128)(2,1)}, bf16[32,16,512]{2,1,0:T(8,128)(2,1)S(1)}, u32[]{:S(2)}) copy-start(bf16[32,16,512]{2,1,0:T(8,128)(2,1)S(1)} %collective-permute-done.5.rest_5_) | copy-start | bytes 1572868
  694.4 36.7 %collective-permute-start.10 = (bf16[32,16,512]{2,1,0:T(8,128)(2,1)}, bf16[32,16,512]{2,1,0:T(8,128)(2,1)S(1)}, u32[]{:S(2)}, u32[]{:S(2)}) collective-permute-start(bf16[32,16,512]{2,1,0:T(8,128)(2,1)} %get-tuple-element.47), channel_id=1, source_target_pairs={{15,10},{14,11},{13,8},{12,9},{11,14},{10,15},{9,12},{8,13},{31,26... | collective-permute-start | bytes 1572872 | tf_op jit(solution)/shard_map/ppermute | solution.py:255
  696.3 56.7 %collective-permute-start.11 = (bf16[32,16,512]{2,1,0:T(8,128)(2,1)}, bf16[32,16,512]{2,1,0:T(8,128)(2,1)}, u32[]{:S(2)}, u32[]{:S(2)}) collective-permute-start(bf16[32,16,512]{2,1,0:T(8,128)(2,1)} %get-tuple-element.48), channel_id=1, source_target_pairs={{15,11},{14,10},{13,9},{12,8},{11,15},{10,14},{9,13},{8,12},{31,27... | collective-permute-start | bytes 1572872 | tf_op jit(solution)/shard_map/ppermute | solution.py:255
  702.6 50.4 %collective-permute-start.12 = (bf16[32,16,512]{2,1,0:T(8,128)(2,1)}, bf16[32,16,512]{2,1,0:T(8,128)(2,1)}, u32[]{:S(2)}, u32[]{:S(2)}) collective-permute-start(bf16[32,16,512]{2,1,0:T(8,128)(2,1)} %get-tuple-element.49), channel_id=1, source_target_pairs={{15,12},{14,13},{13,14},{12,15},{11,8},{10,9},{9,10},{8,11},{31,28... | collective-permute-start | bytes 1572872 | tf_op jit(solution)/shard_map/ppermute | solution.py:255
  707.9 45.2 %collective-permute-start.13 = (bf16[32,16,512]{2,1,0:T(8,128)(2,1)}, bf16[32,16,512]{2,1,0:T(8,128)(2,1)}, u32[]{:S(2)}, u32[]{:S(2)}) collective-permute-start(bf16[32,16,512]{2,1,0:T(8,128)(2,1)} %get-tuple-element.50), channel_id=1, source_target_pairs={{15,13},{14,12},{13,15},{12,14},{11,9},{10,8},{9,11},{8,10},{31,29... | collective-permute-start | bytes 1572872 | tf_op jit(solution)/shard_map/ppermute | solution.py:255
  717.9 35.2 %collective-permute-start.14 = (bf16[32,16,512]{2,1,0:T(8,128)(2,1)}, bf16[32,16,512]{2,1,0:T(8,128)(2,1)}, u32[]{:S(2)}, u32[]{:S(2)}) collective-permute-start(bf16[32,16,512]{2,1,0:T(8,128)(2,1)} %get-tuple-element.51), channel_id=1, source_target_pairs={{15,14},{14,15},{13,12},{12,13},{11,10},{10,11},{9,8},{8,9},{31,30... | collective-permute-start | bytes 1572872 | tf_op jit(solution)/shard_map/ppermute | solution.py:255
  731.0 22.0 %collective-permute-start.15 = (bf16[32,16,512]{2,1,0:T(8,128)(2,1)}, bf16[32,16,512]{2,1,0:T(8,128)(2,1)}, u32[]{:S(2)}, u32[]{:S(2)}) collective-permute-start(bf16[32,16,512]{2,1,0:T(8,128)(2,1)} %get-tuple-element.52), channel_id=1, source_target_pairs={{15,15},{14,14},{13,13},{12,12},{11,11},{10,10},{9,9},{8,8},{31,31... | collective-permute-start | bytes 1572872 | tf_op jit(solution)/shard_map/ppermute | solution.py:255
  (13 other events, 468.9 us)

commit v2 on v0

v2 whole, which is shorter than its diff:
```python
import functools
import math

import jax
import jax.numpy as jnp
import ml_dtypes
import numpy as np
from jax import lax
from jax.experimental import pallas as pl
from jax.experimental.pallas import tpu as pltpu
from jax.sharding import PartitionSpec as P

STAGES = 2
WINDOW = 5
TILE = 16
VMEM_LIMIT = 56 << 20


def fourier_table(nlon, count, per_dev, first, size):
    owner = np.arange(count)[:, None]
    order = (count - 1 - owner) * per_dev + first + np.arange(size)[None, :]
    phase = order[:, :, None] * np.arange(nlon) % nlon
    angle = phase.astype(np.float32) * np.float32(2.0 * math.pi / nlon)
    scale = np.float32(1.0 / math.sqrt(nlon))
    table = np.stack([np.cos(angle) * scale, -np.sin(angle) * scale], axis=1)
    return table.astype(ml_dtypes.bfloat16)


def swap_matrix(outer, inner):
    rows = np.arange(outer * inner)
    source = rows % outer * inner + rows // outer
    return (source[:, None] == rows[None, :]).astype(ml_dtypes.bfloat16)


def fourier_kernel(rows_step, index_ref, table_ref, swap_ref, grid_ref, *rest):
    out_refs, hold = rest[:-1], rest[-1]
    half, _, size, nlon = table_ref.shape
    group, rows, chans = hold.shape
    steps = group // rows_step
    part = lax.rem(pl.program_id(0), steps)
    table = table_ref[...].reshape(rows, nlon)
    for row in range(rows_step):
        result = jnp.dot(table, grid_ref[row], preferred_element_type=jnp.float32)
        hold[part * rows_step + row] = result.astype(jnp.bfloat16)

    @pl.when(part == steps - 1)
    def _():
        for k in range(half):
            owner = jnp.bitwise_xor(lax.rem(index_ref[0], half), k)
            for p in range(2):
                for first in range(0, size, TILE):
                    start = pl.multiple_of((owner * 2 + p) * size + first, TILE)
                    values = hold[:, pl.ds(start, TILE), :].reshape(group * TILE, chans)
                    swapped = jnp.dot(swap_ref[...], values, preferred_element_type=jnp.float32)
                    out_refs[k][first : first + TILE, :, p * chans : (p + 1) * chans] = swapped.astype(
                        jnp.bfloat16
                    ).reshape(TILE, group, chans)


def fourier(index, grid, table, crossing):
    lat_rows, nlon, chans = grid.shape
    count, _, size, _ = table.shape
    half = count // 2
    table = jnp.asarray(table)
    if lat_rows % TILE or size % TILE:
        result = jnp.einsum("ipjn,tnc->ijtpc", table, grid, preferred_element_type=jnp.float32)
        result = result.astype(jnp.bfloat16).reshape(count, size, lat_rows, 2 * chans)
        base = half if crossing else 0
        return [lax.dynamic_index_in_dim(result, index[0] ^ (base + k), keepdims=False) for k in range(half)]
    rows_step = 4
    steps = TILE // rows_step

    def side(g, i):
        mine = i[0] // half
        return (1 - mine if crossing else mine), 0, 0, 0

    rows = 2 * half * size
    return pl.pallas_call(
        functools.partial(fourier_kernel, rows_step),
        out_shape=[jax.ShapeDtypeStruct((size, lat_rows, 2 * chans), jnp.bfloat16)] * half,
        grid_spec=pltpu.PrefetchScalarGridSpec(
            num_scalar_prefetch=1,
            grid=(lat_rows // rows_step,),
            in_specs=[
                pl.BlockSpec((half, 2, size, nlon), side),
                pl.BlockSpec((TILE * TILE, TILE * TILE), lambda g, i: (0, 0)),
                pl.BlockSpec((rows_step, nlon, chans), lambda g, i: (g, 0, 0)),
            ],
            out_specs=[pl.BlockSpec((size, TILE, 2 * chans), lambda g, i: (0, g // steps, 0))] * half,
            scratch_shapes=[pltpu.VMEM((TILE, rows, chans), jnp.bfloat16)],
        ),
        compiler_params=pltpu.CompilerParams(vmem_limit_bytes=VMEM_LIMIT),
        cost_estimate=pl.CostEstimate(
            flops=2 * rows * nlon * chans * lat_rows,
            bytes_accessed=2 * (grid.size + rows * nlon + rows * lat_rows * chans),
            transcendentals=0,
        ),
        name="fourier",
    )(index, table, jnp.asarray(swap_matrix(TILE, TILE)), grid)


def legendre_kernel(skip, index_ref, panel_ref, swap_ref, *rest):
    count = len(rest) // 2 - 1
    spectra_refs, far_refs, values, hold = rest[:count], rest[count:-2], rest[-2], rest[-1]
    degrees, latitudes = panel_ref.shape[2:]
    span, size, width = far_refs[-1].shape
    me = index_ref[0]
    block = count - 1 - me
    j = pl.program_id(0)
    for k in range(count):
        values[jnp.bitwise_xor(me, k)] = spectra_refs[k][0]
    spectra = values[...].reshape(latitudes, width)

    def advance(first):
        part = jnp.dot(panel_ref[0, 0, first:, :], spectra, preferred_element_type=jnp.float32)
        hold[j, first:, :] = part.astype(jnp.bfloat16)

    pl.when(block < count // 2)(functools.partial(advance, 0))
    pl.when(block >= count // 2)(functools.partial(advance, degrees // 2))

    @pl.when(j == size - 1)
    def _():
        for k in range(count):
            degree = jnp.bitwise_xor(block, k)

            @pl.when(degree >= block)
            def _():
                lost = skip if k == 0 else 0
                for first in range(lost, span, TILE):
                    start = pl.multiple_of(degree * span + first, TILE)
                    pieces = hold[:, pl.ds(start, TILE), :].reshape(size * TILE, width)
                    swapped = jnp.dot(swap_ref[...], pieces, preferred_element_type=jnp.float32)
                    far_refs[k][first - lost : first - lost + TILE] = swapped.astype(jnp.bfloat16).reshape(TILE, size, width)


def legendre_part(index, legendre, spectra, first):
    count = len(spectra)
    size, lat_rows, width = spectra[0].shape
    _, panels, degrees, latitudes = legendre.shape
    span = degrees // count
    base = panels // 2 + first
    if size % TILE or span % TILE or lat_rows % TILE:
        values = jnp.take(jnp.stack(spectra), jnp.arange(count) ^ index[0], axis=0)
        values = values.transpose(0, 2, 1, 3).reshape(latitudes, size, width)
        panel = legendre[0, base : base + size]
        result = jnp.einsum("jlt,tjk->ljk", panel, values, preferred_element_type=jnp.float32)
        result = result.astype(jnp.bfloat16).reshape(count, span, size, width)
        block = count - 1 - index[0]
        return [lax.dynamic_index_in_dim(result, block ^ k, keepdims=False) for k in range(count)]
    skip = min(first, span - TILE) // TILE * TILE
    spans = [span - skip] + [span] * (count - 1)
    return pl.pallas_call(
        functools.partial(legendre_kernel, skip),
        out_shape=[jax.ShapeDtypeStruct((rows, size, width), jnp.bfloat16) for rows in spans],
        grid_spec=pltpu.PrefetchScalarGridSpec(
            num_scalar_prefetch=1,
            grid=(size,),
            in_specs=[
                pl.BlockSpec((1, 1, degrees, latitudes), lambda j, i: (0, base + j, 0, 0)),
                pl.BlockSpec((size * TILE, size * TILE), lambda j, i: (0, 0)),
            ]
            + [pl.BlockSpec((1, lat_rows, width), lambda j, i: (j, 0, 0))] * count,
            out_specs=[pl.BlockSpec((rows, size, width), lambda j, i: (0, 0, 0)) for rows in spans],
            scratch_shapes=[
                pltpu.VMEM((count, lat_rows, width), jnp.bfloat16),
                pltpu.VMEM((size, degrees, width), jnp.bfloat16),
            ],
        ),
        compiler_params=pltpu.CompilerParams(vmem_limit_bytes=VMEM_LIMIT),
        cost_estimate=pl.CostEstimate(
            flops=2 * size * degrees * latitudes * width,
            bytes_accessed=2 * size * (degrees * latitudes + 2 * degrees * width),
            transcendentals=0,
        ),
        name="legendre",
    )(index, legendre, jnp.asarray(swap_matrix(size, TILE)), *spectra)


def mixing_kernel(first, count, skips, index_ref, mixing_ref, *rest):
    out_ref, hold = rest[-2:]
    rows, group, size, width = out_ref.shape
    piece_refs = rest[:group]
    chans = width // 2
    me = index_ref[0]
    inside = lax.rem(me, group)

    def advance(row, carry):
        degree = pl.program_id(0) * rows + row
        for n, skip in enumerate(skips):
            where = jnp.bitwise_xor(inside, n)
            piece = piece_refs[n][row]
            if first + n == count - 1:
                piece = jnp.where(jnp.bitwise_xor(me, count - 1) <= me, piece, jnp.zeros_like(piece))
            elif skip:
                piece = jnp.where(degree >= skip, piece, jnp.zeros_like(piece))
            hold[row, 0, where] = piece[:, :chans]
            hold[row, 1, where] = piece[:, chans:]
        values = hold[row].reshape(2 * group * size, chans)
        by_real = jnp.dot(values, mixing_ref[row, 0], preferred_element_type=jnp.float32)
        by_imag = jnp.dot(values, mixing_ref[row, 1], preferred_element_type=jnp.float32)
        half = group * size
        out_real = by_real[:half] - by_imag[half:]
        out_imag = by_imag[:half] + by_real[half:]
        out_ref[row, :, :, :chans] = out_real.astype(jnp.bfloat16).reshape(group, size, chans)
        out_ref[row, :, :, chans:] = out_imag.astype(jnp.bfloat16).reshape(group, size, chans)
        return carry

    lax.fori_loop(0, rows, advance, 0)


def mix_part(index, mixing, pieces, first, count, before, stage, per_dev):
    group = len(pieces)
    span, _, chans, _ = mixing.shape
    size, width = pieces[0].shape[1:]
    skips = [span - piece.shape[0] for piece in pieces]
    step = min(8, span)

    def piece_spec(skip):
        return pl.BlockSpec((step, size, width), lambda l, i: (jnp.maximum(l - skip // step, 0), 0, 0))

    operands = [index, mixing, *pieces]
    specs = [pl.BlockSpec((step, 2, chans, chans), lambda l, i: (l, 0, 0, 0))]
    specs += [piece_spec(skip) for skip in skips]
    aliases = {}
    if before is not None:
        aliases = {len(operands): 0}
        operands.append(before)
        specs.append(pl.BlockSpec(memory_space=pl.ANY))

    def where(l, i):
        return l, jnp.bitwise_xor(i[0], first) // group, stage, 0

    return pl.pallas_call(
        functools.partial(mixing_kernel, first, count, skips),
        out_shape=jax.ShapeDtypeStruct((span, count, per_dev, width), jnp.bfloat16),
        grid_spec=pltpu.PrefetchScalarGridSpec(
            num_scalar_prefetch=1,
            grid=(span // step,),
            in_specs=specs,
            out_specs=pl.BlockSpec((step, group, size, width), where),
            scratch_shapes=[pltpu.VMEM((step, 2, group, size, chans), jnp.bfloat16)],
        ),
        input_output_aliases=aliases,
        compiler_params=pltpu.CompilerParams(vmem_limit_bytes=VMEM_LIMIT),
        cost_estimate=pl.CostEstimate(
            flops=2 * span * group * size * width * width,
            bytes_accessed=2 * (mixing.size + 2 * span * group * size * width),
            transcendentals=0,
        ),
        name="mix",
    )(*operands)


def mix_plain(index, mixing, pieces):
    count = len(pieces)
    stack = jnp.take(jnp.stack(pieces), jnp.arange(count) ^ index[0], axis=0)
    held = jnp.arange(count) <= index[0]
    stack = jnp.where(held[:, None, None, None], stack, jnp.zeros_like(stack))
    real_w, imag_w = mixing[:, 0], mixing[:, 1]
    weight = jnp.concatenate(
        [jnp.concatenate([real_w, imag_w], axis=-1), jnp.concatenate([-imag_w, real_w], axis=-1)], axis=1
    )
    mixed = jnp.einsum("bljk,lkn->lbjn", stack, weight, preferred_element_type=jnp.float32)
    return mixed.astype(jnp.bfloat16)


def weave(stages, half):
    count = 2 * half
    main = [("a", s, k) for s in range(stages) for k in range(half, count)]
    main += [("c", s, k) for s in range(stages) for k in range(half)]
    beside = [[] for _ in main]
    for s in range(stages):
        for n, k in enumerate(range(half - 1, 0, -1)):
            where = s * half + 3 * half // 8 + n if s == 0 else s * half + half // 4 + n
            beside[min(where, len(main) - 1)].append(("a", s, k))
        for n, k in enumerate(range(half, count - 1)):
            where = half + half // 4 + n + s * (half + half // 8)
            beside[min(where, len(main) - 1)].append(("c", s, k))
    order = []
    for first, others in zip(main, beside):
        order.append(first)
        order += others
    return order


def on_device(grid, legendre, mixing):
    count = lax.axis_size("ord")
    half = count // 2
    index = lax.axis_index("ord").astype(jnp.int32).reshape(1)
    nlon = grid.shape[1]
    per_dev = legendre.shape[1] // 2
    stages = STAGES if per_dev % (STAGES * TILE) == 0 else 1
    size = per_dev // stages
    tables = [fourier_table(nlon, count, per_dev, s * size, size) for s in range(stages)]
    sends = {}
    landed = {}
    recent = []

    def after(value, key):
        value, landed[key] = lax.optimization_barrier((value, landed[key]))
        return value

    def spectra_to_send(stage, k):
        crossing = k >= half
        if (stage, crossing) not in sends:
            token = after(index, recent[-WINDOW]) if len(recent) >= WINDOW else index
            sends[stage, crossing] = fourier(token, grid, tables[stage], crossing)
        return sends[stage, crossing][k % half]

    coeffs = {}

    def coeffs_to_send(stage, k):
        if stage not in coeffs:
            for other in range(count):
                if ("a", stage, other) not in landed:
                    permute("a", stage, other)
            spectra = [landed["a", stage, other] for other in range(count)]
            coeffs[stage] = list(legendre_part(index, legendre, spectra, stage * size))
        return coeffs[stage][k]

    def permute(kind, stage, k):
        key = (kind, stage, k)
        if key in landed:
            return
        value = spectra_to_send(stage, k) if kind == "a" else coeffs_to_send(stage, k)
        if (kind == "a" and k == 0) or (kind == "c" and k == count - 1):
            landed[key] = value
            return
        if len(recent) >= WINDOW:
            value = after(value, recent[-WINDOW])
        if kind == "a":
            pairs = [(i, i ^ k) for i in range(count)]
        else:
            pairs = [(count - 1 - b, b ^ k) for b in range(count) if b ^ k >= b]
        landed[key] = lax.ppermute(value, "ord", pairs)
        recent.append(key)

    out = None
    mixed = [0] * stages
    done = []
    whole, split = [(0, count)], [(half, half), (0, half)]
    groups = [whole] * (stages - 1) + [split]

    def mix_ready(limit):
        nonlocal out
        for stage in range(stages):
            while stages > 1 and mixed[stage] < len(groups[stage]):
                first, group = groups[stage][mixed[stage]]
                keys = [("c", stage, k) for k in range(first, first + group)]
                if any(key in recent[limit:] or key not in landed for key in keys if key[2] != count - 1):
                    return
                mixed[stage] += 1
                if ("c", stage, count - 1) in keys:
                    permute("c", stage, count - 1)
                pieces = [landed[key] for key in keys]
                out = mix_part(index, mixing, pieces, first, count, out, stage, per_dev)
                done.append(len(recent))

    for kind, stage, k in weave(stages, half):
        mix_ready(max(len(recent) - WINDOW, 0))
        if done and kind == "c" and done[-1] == len(recent) and k < half:
            coeffs_to_send(stage, k)
            coeffs[stage][k], out = lax.optimization_barrier((coeffs[stage][k], out))
        permute(kind, stage, k)
    mix_ready(len(recent))
    if stages == 1:
        permute("c", 0, count - 1)
        out = mix_plain(index, mixing, [landed["c", 0, k] for k in range(count)])
    span, _, _, width = out.shape
    return out.reshape(span, count * per_dev, width)


def solution(mesh):
    return jax.shard_map(
        on_device,
        mesh=mesh,
        in_specs=(
            P(("grp", "ord"), None, None),
            P("ord", None, None, None),
            P("ord", None, None, None),
        ),
        out_specs=P(("grp", "ord"), None, None),
        check_vma=False,
    )
```

time: 921 us -> 714 us (0.78)
  waiting for transfers between devices: 696 us -> 400 us
  starting transfers between devices: 26.4 us -> 167 us
  Pallas kernels: 0 us -> 136 us
  local copies, waits for them, and re-layouts: 113 us -> 4.89 us
  matrix products: 68.3 us -> 0 us
  other arithmetic: 13.2 us -> 0 us
    all_to_all x2 -> x0, waiting for transfers between devices: 696 us -> none  [the longest x1 350 us: on_device(): lax.all_to_all(coeffs, 'ord', split_axis=1, concat_axis=0, tiled=True)]
    ppermute x0 -> x60, waiting for transfers between devices: none -> 400 us  [permute(): landed[key] = lax.ppermute(value, 'ord', pairs)]
    ppermute x0 -> x60, starting transfers between devices: none -> 167 us  [permute(): landed[key] = lax.ppermute(value, 'ord', pairs)]
    pallas_call x0 -> x9, Pallas kernels: none -> 136 us  [the longest x4 56.3 us: fourier(): pl.pallas_call(functools.partial(fourier_kernel, rows_step), out_shape=[j...]
    dot_general x4 -> x0, matrix products: 68.3 us -> none  [the longest x1 25.9 us: on_device(): jnp.einsum('tnc,nk->tkc', grid, table, preferred_element_type=jnp.float32)]
    reshape x2 -> x0, local copies, waits for them, and re-layouts: 43 us -> none  [on_device(): sending = spectra.reshape(lat_rows, orders, 2 * chans)]
    all_to_all x2 -> x0, local copies, waits for them, and re-layouts: 28.5 us -> none  [the longest x1 14.4 us: on_device(): lax.all_to_all(coeffs, 'ord', split_axis=1, concat_axis=0, tiled=True)]
    all_to_all x2 -> x0, starting transfers between devices: 26.4 us -> none  [the longest x1 20 us: on_device(): lax.all_to_all(coeffs, 'ord', split_axis=1, concat_axis=0, tiled=True)]
  transfers between devices with their start and end apart: 2 -> 60, of which waited for: 2 -> 22; matrix products, arithmetic and copies ran while one was open for 3% -> 0% of each run, Pallas kernels for 0% -> 16%
where the time goes in v2:
time: 714 us; the launch traced here: 709 us
  waiting for transfers between devices  400 us (56%)
  starting transfers between devices  167 us (23%)
  Pallas kernels  136 us (19%)
    ppermute x60, waiting for transfers between devices, permute(): landed[key] = lax.ppermute(value, 'ord', pairs)  400 us
    ppermute x60, starting transfers between devices, permute(): landed[key] = lax.ppermute(value, 'ord', pairs)  167 us
    pallas_call x4, Pallas kernels, fourier(): pl.pallas_call(functools.partial(fourier_kernel, rows_step), out_shape=[j...  56.3 us
    pallas_call x2, Pallas kernels, legendre_part(): pl.pallas_call(functools.partial(legendre_kernel, skip), out_shape=[jax.S...  44.2 us
    pallas_call x3, Pallas kernels, mix_part(): pl.pallas_call(functools.partial(mixing_kernel, first, count, skips), out...  35.8 us
  transfers between devices with their start and end apart: 60, of which 22 were waited for; matrix products, arithmetic and copies ran while one was open for 0% of the time, Pallas kernels for 16%

profile of v2, /device:TPU:21, one launch (start us, length us, event | category | flops | bytes accessed | tf_op | source)
XLA Modules:
  0.0 708.8 jit_solution(13657255087179728730)
XLA Ops:
  0.0 14.1 %fourier.5 = (bf16[16,32,512]{2,1,0:T(8,128)(2,1)}, bf16[16,32,512]{2,1,0:T(8,128)(2,1)}, bf16[16,32,512]{2,1,0:T(8,128)(2,1)}, bf16[16,32,512]{2,1,0:T(8,128)(2...) custom-call(s32[1]{0:T(128)} %bitcast.index_ref, ...), custom_call_target="tpu_custom_call" | custom-call | flops 4294967296 | bytes 21495808 | tf_op jit(solution)/shard_map/fourier/pallas_call | solution.py:78
  17.0 14.0 %fourier.4 = (bf16[16,32,512]{2,1,0:T(8,128)(2,1)}, bf16[16,32,512]{2,1,0:T(8,128)(2,1)}, bf16[16,32,512]{2,1,0:T(8,128)(2,1)}, bf16[16,32,512]{2,1,0:T(8,128)(2...) custom-call(s32[1]{0:T(128)} %bitcast.index_ref, ...), custom_call_target="tpu_custom_call" | custom-call | flops 4294967296 | bytes 21495808 | tf_op jit(solution)/shard_map/fourier/pallas_call | solution.py:78
  33.7 15.4 %collective-permute-done.5.rest_9_ = bf16[16,32,512]{2,1,0:T(8,128)(2,1)S(1)} collective-permute-done((bf16[16,32,512]{2,1,0:T(8,128)(2,1)}, bf16[16,32,512]{2,1,0:T(8,128)(2,1)S(1)}, u32[]{:S(2)}, u32[]{:S(2)}) %collective-permute-start.5) | collective-permute-done | bytes 524320 | tf_op jit(solution)/shard_map/ppermute | solution.py:335
  49.1 4.3 collective-permute-start.6
  54.3 17.3 %collective-permute-done.9.rest_10_ = bf16[16,32,512]{2,1,0:T(8,128)(2,1)S(1)} collective-permute-done((bf16[16,32,512]{2,1,0:T(8,128)(2,1)}, bf16[16,32,512]{2,1,0:T(8,128)(2,1)S(1)}, u32[]{:S(2)}, u32[]{:S(2)}) %collective-permute-start.9) | collective-permute-done | bytes 524320 | tf_op jit(solution)/shard_map/ppermute | solution.py:335
  71.6 2.8 collective-permute-start.10
  74.6 41.9 %collective-permute-done.12.rest_8_ = bf16[16,32,512]{2,1,0:T(8,128)(2,1)S(1)} collective-permute-done((bf16[16,32,512]{2,1,0:T(8,128)(2,1)S(1)}, bf16[16,32,512]{2,1,0:T(8,128)(2,1)S(1)}, u32[]{:S(2)}, u32[]{:S(2)}) %collective-permute-start.12) | collective-permute-done | bytes 524320 | tf_op jit(solution)/shard_map/ppermute | solution.py:335
  116.5 2.6 collective-permute-start.13
  119.3 30.8 %collective-permute-done.3.rest_11_ = bf16[16,32,512]{2,1,0:T(8,128)(2,1)S(1)} collective-permute-done((bf16[16,32,512]{2,1,0:T(8,128)(2,1)S(1)}, bf16[16,32,512]{2,1,0:T(8,128)(2,1)S(1)}, u32[]{:S(2)}, u32[]{:S(2)}) %collective-permute-start.3) | collective-permute-done | bytes 524320 | tf_op jit(solution)/shard_map/ppermute | solution.py:335
  150.2 4.7 collective-permute-start.4
  154.9 9.8 %collective-permute-done.10.rest_13_ = bf16[16,32,512]{2,1,0:T(8,128)(2,1)S(1)} collective-permute-done((bf16[16,32,512]{2,1,0:T(8,128)(2,1)S(1)}, bf16[16,32,512]{2,1,0:T(8,128)(2,1)S(1)}, u32[]{:S(2)}, u32[]{:S(2)}) %collective-permute-start.10) | collective-permute-done | bytes 524320 | tf_op jit(solution)/shard_map/ppermute | solution.py:335
  164.7 11.2 %collective-permute-done.1.rest_14_ = bf16[16,32,512]{2,1,0:T(8,128)(2,1)S(1)} collective-permute-done((bf16[16,32,512]{2,1,0:T(8,128)(2,1)S(1)}, bf16[16,32,512]{2,1,0:T(8,128)(2,1)S(1)}, u32[]{:S(2)}, u32[]{:S(2)}) %collective-permute-start.1) | collective-permute-done | bytes 524320 | tf_op jit(solution)/shard_map/ppermute | solution.py:335
  177.9 9.3 %collective-permute-done.13.rest_12_ = bf16[16,32,512]{2,1,0:T(8,128)(2,1)S(1)} collective-permute-done((bf16[16,32,512]{2,1,0:T(8,128)(2,1)S(1)}, bf16[16,32,512]{2,1,0:T(8,128)(2,1)S(1)}, u32[]{:S(2)}, u32[]{:S(2)}) %collective-permute-start.13) | collective-permute-done | bytes 524320 | tf_op jit(solution)/shard_map/ppermute | solution.py:335
  187.2 11.2 %collective-permute-done.7.rest_15_ = bf16[16,32,512]{2,1,0:T(8,128)(2,1)S(1)} collective-permute-done((bf16[16,32,512]{2,1,0:T(8,128)(2,1)S(1)}, bf16[16,32,512]{2,1,0:T(8,128)(2,1)S(1)}, u32[]{:S(2)}, u32[]{:S(2)}) %collective-permute-start.7) | collective-permute-done | bytes 524320 | tf_op jit(solution)/shard_map/ppermute | solution.py:335
  198.9 14.2 %fourier.7 = (bf16[16,32,512]{2,1,0:T(8,128)(2,1)}, bf16[16,32,512]{2,1,0:T(8,128)(2,1)}, bf16[16,32,512]{2,1,0:T(8,128)(2,1)}, bf16[16,32,512]{2,1,0:T(8,128)(2...) custom-call(s32[1]{0:T(128)} %bitcast.index_ref, ...), custom_call_target="tpu_custom_call" | custom-call | flops 4294967296 | bytes 21495808 | tf_op jit(solution)/shard_map/fourier/pallas_call | solution.py:78
  214.0 3.3 collective-permute-start.15
  217.4 22.2 %legendre.2 = (bf16[32,16,512]{2,1,0:T(8,128)(2,1)}, bf16[32,16,512]{2,1,0:T(8,128)(2,1)}, bf16[32,16,512]{2,1,0:T(8,128)(2,1)}, bf16[32,16,512]{2,1,0:T(8,128)(...) custom-call(s32[1]{0:T(128)} %bitcast.index_ref, ...), custom_call_target="tpu_custom_call" | custom-call | flops 4294967296 | bytes 25165824 | tf_op jit(solution)/shard_map/legendre/pallas_call | solution.py:152
  239.7 7.7 %collective-permute-done.27.rest_8_ = bf16[16,32,512]{2,1,0:T(8,128)(2,1)S(1)} collective-permute-done((bf16[16,32,512]{2,1,0:T(8,128)(2,1)}, bf16[16,32,512]{2,1,0:T(8,128)(2,1)S(1)}, u32[]{:S(2)}, u32[]{:S(2)}) %collective-permute-start.27) | collective-permute-done | bytes 524320 | tf_op jit(solution)/shard_map/ppermute | solution.py:335
  247.4 4.4 collective-permute-start.28
  251.7 14.0 %fourier.6 = (bf16[16,32,512]{2,1,0:T(8,128)(2,1)}, bf16[16,32,512]{2,1,0:T(8,128)(2,1)}, bf16[16,32,512]{2,1,0:T(8,128)(2,1)}, bf16[16,32,512]{2,1,0:T(8,128)(2...) custom-call(s32[1]{0:T(128)} %bitcast.index_ref, ...), custom_call_target="tpu_custom_call" | custom-call | flops 4294967296 | bytes 21495808 | tf_op jit(solution)/shard_map/fourier/pallas_call | solution.py:78
  267.8 2.6 collective-permute-start.24
  270.7 17.8 %collective-permute-done.20.rest_7_ = bf16[16,32,512]{2,1,0:T(8,128)(2,1)S(1)} collective-permute-done((bf16[16,32,512]{2,1,0:T(8,128)(2,1)}, bf16[16,32,512]{2,1,0:T(8,128)(2,1)S(1)}, u32[]{:S(2)}, u32[]{:S(2)}) %collective-permute-start.20) | collective-permute-done | bytes 524320 | tf_op jit(solution)/shard_map/ppermute | solution.py:335
  288.6 5.2 collective-permute-start.21
  293.9 20.1 %collective-permute-done.16.rest_6_ = bf16[16,32,512]{2,1,0:T(8,128)(2,1)S(1)} collective-permute-done((bf16[16,32,512]{2,1,0:T(8,128)(2,1)}, bf16[16,32,512]{2,1,0:T(8,128)(2,1)S(1)}, u32[]{:S(2)}, u32[]{:S(2)}) %collective-permute-start.16) | collective-permute-done | bytes 524320 | tf_op jit(solution)/shard_map/ppermute | solution.py:335
  314.0 4.8 collective-permute-start.17
  318.8 6.4 collective-permute-done.24.rest_9_
  328.1 30.9 %collective-permute-done.21.rest_10_ = bf16[32,16,512]{2,1,0:T(8,128)(2,1)S(1)} collective-permute-done((bf16[32,16,512]{2,1,0:T(8,128)(2,1)}, bf16[32,16,512]{2,1,0:T(8,128)(2,1)S(1)}, u32[]{:S(2)}, u32[]{:S(2)}) %collective-permute-start.21) | collective-permute-done | bytes 524320 | tf_op jit(solution)/shard_map/ppermute | solution.py:335
  361.4 20.0 %collective-permute-done.17.rest_11_ = bf16[32,16,512]{2,1,0:T(8,128)(2,1)S(1)} collective-permute-done((bf16[32,16,512]{2,1,0:T(8,128)(2,1)}, bf16[32,16,512]{2,1,0:T(8,128)(2,1)S(1)}, u32[]{:S(2)}, u32[]{:S(2)}) %collective-permute-start.17) | collective-permute-done | bytes 524320 | tf_op jit(solution)/shard_map/ppermute | solution.py:335
  382.7 21.3 %collective-permute-done.30.rest_4_ = bf16[16,32,512]{2,1,0:T(8,128)(2,1)S(1)} collective-permute-done((bf16[16,32,512]{2,1,0:T(8,128)(2,1)}, bf16[16,32,512]{2,1,0:T(8,128)(2,1)S(1)}, u32[]{:S(2)}, u32[]{:S(2)}) %collective-permute-start.30) | collective-permute-done | bytes 524320 | tf_op jit(solution)/shard_map/ppermute | solution.py:335
  403.9 2.8 collective-permute-start.44
  407.4 7.8 %collective-permute-done.33.rest_5_ = bf16[16,32,512]{2,1,0:T(8,128)(2,1)S(1)} collective-permute-done((bf16[16,32,512]{2,1,0:T(8,128)(2,1)}, bf16[16,32,512]{2,1,0:T(8,128)(2,1)S(1)}, u32[]{:S(2)}, u32[]{:S(2)}) %collective-permute-start.33) | collective-permute-done | bytes 524320 | tf_op jit(solution)/shard_map/ppermute | solution.py:335
  415.2 3.0 collective-permute-start.34
  422.7 10.5 %collective-permute-done.23.rest_2_ = bf16[16,32,512]{2,1,0:T(8,128)(2,1)S(1)} collective-permute-done((bf16[16,32,512]{2,1,0:T(8,128)(2,1)}, bf16[16,32,512]{2,1,0:T(8,128)(2,1)S(1)}, u32[]{:S(2)}, u32[]{:S(2)}) %collective-permute-start.23) | collective-permute-done | bytes 524320 | tf_op jit(solution)/shard_map/ppermute | solution.py:335
  435.1 12.9 %collective-permute-done.34.rest_12_ = bf16[32,16,512]{2,1,0:T(8,128)(2,1)S(1)} collective-permute-done((bf16[32,16,512]{2,1,0:T(8,128)(2,1)}, bf16[32,16,512]{2,1,0:T(8,128)(2,1)S(1)}, u32[]{:S(2)}, u32[]{:S(2)}) %collective-permute-start.34) | collective-permute-done | bytes 524320 | tf_op jit(solution)/shard_map/ppermute | solution.py:335
  449.0 22.0 %legendre.3 = (bf16[16,16,512]{2,1,0:T(8,128)(2,1)}, bf16[32,16,512]{2,1,0:T(8,128)(2,1)}, bf16[32,16,512]{2,1,0:T(8,128)(2,1)}, bf16[32,16,512]{2,1,0:T(8,128)(...) custom-call(s32[1]{0:T(128)} %bitcast.index_ref, ...), custom_call_target="tpu_custom_call" | custom-call | flops 4294967296 | bytes 25165824 | tf_op jit(solution)/shard_map/legendre/pallas_call | solution.py:152
  471.1 4.4 collective-permute-start.43
  476.3 3.7 collective-permute-start.46
  480.7 9.3 %collective-permute-start.36 = (bf16[32,16,512]{2,1,0:T(8,128)(2,1)}, bf16[32,16,512]{2,1,0:T(8,128)(2,1)S(1)}, u32[]{:S(2)}, u32[]{:S(2)}) collective-permute-start(bf16[32,16,512]{2,1,0:T(8,128)(2,1)} %get-tuple-element.287), channel_id=1, source_target_pairs={{15,3},{14,2},{11,7},{10,6},{7,11},{6,10},{3,15},{2,14},{31,19},{3... | collective-permute-start | bytes 1572872 | tf_op jit(solution)/shard_map/ppermute | solution.py:335
  490.7 33.0 %collective-permute-start.40 = (bf16[32,16,512]{2,1,0:T(8,128)(2,1)}, bf16[32,16,512]{2,1,0:T(8,128)(2,1)S(1)}, u32[]{:S(2)}, u32[]{:S(2)}) collective-permute-start(bf16[32,16,512]{2,1,0:T(8,128)(2,1)} %get-tuple-element.296), channel_id=1, source_target_pairs={{15,11},{14,10},{13,9},{12,8},{11,15},{10,14},{9,13},{8,12},{31,27... | collective-permute-start | bytes 1572872 | tf_op jit(solution)/shard_map/ppermute | solution.py:335
  523.7 8.5 %collective-permute-done.46.rest_1_ = bf16[32,16,512]{2,1,0:T(8,128)(2,1)S(1)} collective-permute-done((bf16[32,16,512]{2,1,0:T(8,128)(2,1)}, bf16[32,16,512]{2,1,0:T(8,128)(2,1)S(1)}, u32[]{:S(2)}, u32[]{:S(2)}) %collective-permute-start.46) | collective-permute-done | bytes 524320 | tf_op jit(solution)/shard_map/ppermute | solution.py:335
  534.9 7.2 %collective-permute-start.37 = (bf16[32,16,512]{2,1,0:T(8,128)(2,1)}, bf16[32,16,512]{2,1,0:T(8,128)(2,1)S(1)}, u32[]{:S(2)}, u32[]{:S(2)}) collective-permute-start(bf16[32,16,512]{2,1,0:T(8,128)(2,1)} %get-tuple-element.288), channel_id=1, source_target_pairs={{15,10},{14,11},{13,8},{12,9},{11,14},{10,15},{9,12},{8,13},{31,26... | collective-permute-start | bytes 1572872 | tf_op jit(solution)/shard_map/ppermute | solution.py:335
  542.1 25.3 %collective-permute-start.52 = (bf16[32,16,512]{2,1,0:T(8,128)(2,1)}, bf16[32,16,512]{2,1,0:T(8,128)(2,1)S(1)}, u32[]{:S(2)}, u32[]{:S(2)}) collective-permute-start(bf16[32,16,512]{2,1,0:T(8,128)(2,1)} %get-tuple-element.343), channel_id=1, source_target_pairs={{15,13},{14,12},{13,15},{12,14},{11,9},{10,8},{9,11},{8,10},{31,29... | collective-permute-start | bytes 1572872 | tf_op jit(solution)/shard_map/ppermute | solution.py:335
  572.2 14.1 %mix.3.rest_8_ = bf16[32,16,32,512]{3,2,1,0:T(8,128)(2,1)} custom-call(s32[1]{0:T(128)} %bitcast.index_ref, bf16[32,2,256,256]{3,2,1,0:T(8,128)(2,1)} %mixing_ref.5, bf16[32,16,512]{2,1,0:T(8,128)(2,1)} %collective-permute-done.35.rest_0_, bf16[32,16,512]{2,1,0:T(8,128)(2,1)} %copy-done.13, bf16[32,16,512]{2,1,0:T(8,128)(2,1)} %copy-done.17, ...), custom_call_target="tpu_custom_call" | custom-call | flops 4294967296 | bytes 25165824 | tf_op jit(solution)/shard_map/mix/pallas_call | solution.py:233
  586.3 5.7 collective-permute-start.54
  592.2 45.3 %collective-permute-done.38.rest_0_ = bf16[16,16,512]{2,1,0:T(8,128)(2,1)S(1)} collective-permute-done((bf16[16,16,512]{2,1,0:T(8,128)(2,1)S(1)}, bf16[16,16,512]{2,1,0:T(8,128)(2,1)S(1)}, u32[]{:S(2)}, u32[]{:S(2)}) %collective-permute-start.38) | collective-permute-done | bytes 262176 | tf_op jit(solution)/shard_map/ppermute | solution.py:335
  642.0 10.9 %mix.4.rest_8_ = bf16[32,16,32,512]{3,2,1,0:T(8,128)(2,1)} custom-call(s32[1]{0:T(128)} %bitcast.index_ref, bf16[32,2,256,256]{3,2,1,0:T(8,128)(2,1)} %mixing_ref.5, bf16[32,16,512]{2,1,0:T(8,128)(2,1)} %copy-done.15, bf16[32,16,512]{2,1,0:T(8,128)(2,1)} %copy-done.19, bf16[32,16,512]{2,1,0:T(8,128)(2,1)} %copy-done.39, ...), custom_call_target="tpu_custom_call", output_to_operand_aliasing={{}: (10, {})} | custom-call | flops 2147483648 | bytes 16777216 | tf_op jit(solution)/shard_map/mix/pallas_call | solution.py:233
  653.7 42.1 %collective-permute-done.55.rest_3_ = bf16[32,16,512]{2,1,0:T(8,128)(2,1)S(1)} collective-permute-done((bf16[32,16,512]{2,1,0:T(8,128)(2,1)}, bf16[32,16,512]{2,1,0:T(8,128)(2,1)S(1)}, u32[]{:S(2)}, u32[]{:S(2)}) %collective-permute-start.55) | collective-permute-done | bytes 524320 | tf_op jit(solution)/shard_map/ppermute | solution.py:335
  698.0 10.8 %mix.5 = bf16[32,16,32,512]{3,2,1,0:T(8,128)(2,1)} custom-call(s32[1]{0:T(128)} %bitcast.index_ref, bf16[32,2,256,256]{3,2,1,0:T(8,128)(2,1)} %mixing_ref.5, bf16[16,16,512]{2,1,0:T(8,128)(2,1)} %copy-done.57, bf16[32,16,512]{2,1,0:T(8,128)(2,1)} %copy-done.31, bf16[32,16,512]{2,1,0:T(8,128)(2,1)} %copy-done.45, ...), custom_call_target="tpu_custom_call", output_to_operand_aliasing={{}: (10, {})} | custom-call | flops 2147483648 | bytes 16777216 | tf_op jit(solution)/shard_map/mix/pallas_call | solution.py:233
  (223 shorter events, 44.0 us)
Async XLA Ops:
  14.1 35.0 %collective-permute-start.5 = (bf16[16,32,512]{2,1,0:T(8,128)(2,1)}, bf16[16,32,512]{2,1,0:T(8,128)(2,1)S(1)}, u32[]{:S(2)}, u32[]{:S(2)}) collective-permute-start(bf16[16,32,512]{2,1,0:T(8,128)(2,1)} %get-tuple-element.199), channel_id=1, source_target_pairs={{0,9},{1,8},{2,11},{3,10},{4,13},{5,12},{6,15},{7,14},{8,1},{9,0},... | collective-permute-start | bytes 1572872 | tf_op jit(solution)/shard_map/ppermute | solution.py:335
  14.8 56.8 %collective-permute-start.9 = (bf16[16,32,512]{2,1,0:T(8,128)(2,1)}, bf16[16,32,512]{2,1,0:T(8,128)(2,1)S(1)}, u32[]{:S(2)}, u32[]{:S(2)}) collective-permute-start(bf16[16,32,512]{2,1,0:T(8,128)(2,1)} %get-tuple-element.206), channel_id=1, source_target_pairs={{0,10},{1,11},{2,8},{3,9},{4,14},{5,15},{6,12},{7,13},{8,2},{9,3},... | collective-permute-start | bytes 1572872 | tf_op jit(solution)/shard_map/ppermute | solution.py:335
  31.0 43.4 %collective-permute-start = (bf16[16,32,512]{2,1,0:T(8,128)(2,1)}, bf16[16,32,512]{2,1,0:T(8,128)(2,1)S(1)}, u32[]{:S(2)}, u32[]{:S(2)}) collective-permute-start(bf16[16,32,512]{2,1,0:T(8,128)(2,1)} %get-tuple-element.184), channel_id=1, source_target_pairs={{0,7},{1,6},{2,5},{3,4},{4,3},{5,2},{6,1},{7,0},{8,15},{9,14},{10,... | collective-permute-start | bytes 1572872 | tf_op jit(solution)/shard_map/ppermute | solution.py:335
  33.3 83.1 %collective-permute-start.12 = (bf16[16,32,512]{2,1,0:T(8,128)(2,1)S(1)}, bf16[16,32,512]{2,1,0:T(8,128)(2,1)S(1)}, u32[]{:S(2)}, u32[]{:S(2)}) collective-permute-start(bf16[16,32,512]{2,1,0:T(8,128)(2,1)S(1)} %copy-done.69), channel_id=1, source_target_pairs={{0,8},{1,9},{2,10},{3,11},{4,12},{5,13},{6,14},{7,15},{8,0},{9,1},... | collective-permute-start | bytes 1572872 | tf_op jit(solution)/shard_map/ppermute | solution.py:335
  49.1 69.9 %collective-permute-start.6 = (bf16[16,32,512]{2,1,0:T(8,128)(2,1)}, bf16[16,32,512]{2,1,0:T(8,128)(2,1)S(1)}, u32[]{:S(2)}, u32[]{:S(2)}) collective-permute-start(bf16[16,32,512]{2,1,0:T(8,128)(2,1)} %get-tuple-element.200), channel_id=1, source_target_pairs={{0,6},{1,7},{2,4},{3,5},{4,2},{5,3},{6,0},{7,1},{8,14},{9,15},{10,... | collective-permute-start | bytes 1572872 | tf_op jit(solution)/shard_map/ppermute | solution.py:335
  53.4 96.7 %collective-permute-start.3 = (bf16[16,32,512]{2,1,0:T(8,128)(2,1)S(1)}, bf16[16,32,512]{2,1,0:T(8,128)(2,1)S(1)}, u32[]{:S(2)}, u32[]{:S(2)}) collective-permute-start(bf16[16,32,512]{2,1,0:T(8,128)(2,1)S(1)} %copy-done.68), channel_id=1, source_target_pairs={{0,11},{1,10},{2,9},{3,8},{4,15},{5,14},{6,13},{7,12},{8,3},{9,2},... | collective-permute-start | bytes 1572872 | tf_op jit(solution)/shard_map/ppermute | solution.py:335
  71.6 93.1 %collective-permute-start.10 = (bf16[16,32,512]{2,1,0:T(8,128)(2,1)S(1)}, bf16[16,32,512]{2,1,0:T(8,128)(2,1)S(1)}, u32[]{:S(2)}, u32[]{:S(2)}) collective-permute-start(bf16[16,32,512]{2,1,0:T(8,128)(2,1)S(1)} %copy-done.67), channel_id=1, source_target_pairs={{0,13},{1,12},{2,15},{3,14},{4,9},{5,8},{6,11},{7,10},{8,5},{9,4},... | collective-permute-start | bytes 1572872 | tf_op jit(solution)/shard_map/ppermute | solution.py:335
  74.5 101.4 %collective-permute-start.1 = (bf16[16,32,512]{2,1,0:T(8,128)(2,1)S(1)}, bf16[16,32,512]{2,1,0:T(8,128)(2,1)S(1)}, u32[]{:S(2)}, u32[]{:S(2)}) collective-permute-start(bf16[16,32,512]{2,1,0:T(8,128)(2,1)S(1)} %copy-done.66), channel_id=1, source_target_pairs={{0,14},{1,15},{2,12},{3,13},{4,10},{5,11},{6,8},{7,9},{8,6},{9,7},... | collective-permute-start | bytes 1572872 | tf_op jit(solution)/shard_map/ppermute | solution.py:335
  116.5 70.7 %collective-permute-start.13 = (bf16[16,32,512]{2,1,0:T(8,128)(2,1)S(1)}, bf16[16,32,512]{2,1,0:T(8,128)(2,1)S(1)}, u32[]{:S(2)}, u32[]{:S(2)}) collective-permute-start(bf16[16,32,512]{2,1,0:T(8,128)(2,1)S(1)} %copy-done.65), channel_id=1, source_target_pairs={{0,12},{1,13},{2,14},{3,15},{4,8},{5,9},{6,10},{7,11},{8,4},{9,5},... | collective-permute-start | bytes 1572872 | tf_op jit(solution)/shard_map/ppermute | solution.py:335
  119.0 79.4 %collective-permute-start.7 = (bf16[16,32,512]{2,1,0:T(8,128)(2,1)S(1)}, bf16[16,32,512]{2,1,0:T(8,128)(2,1)S(1)}, u32[]{:S(2)}, u32[]{:S(2)}) collective-permute-start(bf16[16,32,512]{2,1,0:T(8,128)(2,1)S(1)} %copy-done.63), channel_id=1, source_target_pairs={{0,15},{1,14},{2,13},{3,12},{4,11},{5,10},{6,9},{7,8},{8,7},{9,6},... | collective-permute-start | bytes 1572872 | tf_op jit(solution)/shard_map/ppermute | solution.py:335
  150.2 48.7 %collective-permute-start.4 = (bf16[16,32,512]{2,1,0:T(8,128)(2,1)}, bf16[16,32,512]{2,1,0:T(8,128)(2,1)S(1)}, u32[]{:S(2)}, u32[]{:S(2)}) collective-permute-start(bf16[16,32,512]{2,1,0:T(8,128)(2,1)} %get-tuple-element.192), channel_id=1, source_target_pairs={{0,5},{1,4},{2,7},{3,6},{4,1},{5,0},{6,3},{7,2},{8,13},{9,12},{10,... | collective-permute-start | bytes 1572872 | tf_op jit(solution)/shard_map/ppermute | solution.py:335
  175.9 37.2 %collective-permute-start.2 = (bf16[16,32,512]{2,1,0:T(8,128)(2,1)}, bf16[16,32,512]{2,1,0:T(8,128)(2,1)S(1)}, u32[]{:S(2)}, u32[]{:S(2)}) collective-permute-start(bf16[16,32,512]{2,1,0:T(8,128)(2,1)} %get-tuple-element.186), channel_id=1, source_target_pairs={{0,2},{1,3},{2,0},{3,1},{4,6},{5,7},{6,4},{7,5},{8,10},{9,11},{10,... | collective-permute-start | bytes 1572872 | tf_op jit(solution)/shard_map/ppermute | solution.py:335
  177.1 36.0 %collective-permute-start.11 = (bf16[16,32,512]{2,1,0:T(8,128)(2,1)}, bf16[16,32,512]{2,1,0:T(8,128)(2,1)S(1)}, u32[]{:S(2)}, u32[]{:S(2)}) collective-permute-start(bf16[16,32,512]{2,1,0:T(8,128)(2,1)} %get-tuple-element.208), channel_id=1, source_target_pairs={{0,3},{1,2},{2,1},{3,0},{4,7},{5,6},{6,5},{7,4},{8,11},{9,10},{10,... | collective-permute-start | bytes 1572872 | tf_op jit(solution)/shard_map/ppermute | solution.py:335
  213.1 34.3 %collective-permute-start.27 = (bf16[16,32,512]{2,1,0:T(8,128)(2,1)}, bf16[16,32,512]{2,1,0:T(8,128)(2,1)S(1)}, u32[]{:S(2)}, u32[]{:S(2)}) collective-permute-start(bf16[16,32,512]{2,1,0:T(8,128)(2,1)} %get-tuple-element.258), channel_id=1, source_target_pairs={{0,8},{1,9},{2,10},{3,11},{4,12},{5,13},{6,14},{7,15},{8,0},{9,1},... | collective-permute-start | bytes 1572872 | tf_op jit(solution)/shard_map/ppermute | solution.py:335
  214.0 52.0 %collective-permute-start.15 = (bf16[16,32,512]{2,1,0:T(8,128)(2,1)}, bf16[16,32,512]{2,1,0:T(8,128)(2,1)S(1)}, u32[]{:S(2)}, u32[]{:S(2)}) collective-permute-start(bf16[16,32,512]{2,1,0:T(8,128)(2,1)} %get-tuple-element.232), channel_id=1, source_target_pairs={{0,10},{1,11},{2,8},{3,9},{4,14},{5,15},{6,12},{7,13},{8,2},{9,3},... | collective-permute-start | bytes 1572872 | tf_op jit(solution)/shard_map/ppermute | solution.py:335
  266.0 48.0 %collective-permute-start.16 = (bf16[16,32,512]{2,1,0:T(8,128)(2,1)}, bf16[16,32,512]{2,1,0:T(8,128)(2,1)S(1)}, u32[]{:S(2)}, u32[]{:S(2)}) collective-permute-start(bf16[16,32,512]{2,1,0:T(8,128)(2,1)} %get-tuple-element.233), channel_id=1, source_target_pairs={{0,6},{1,7},{2,4},{3,5},{4,2},{5,3},{6,0},{7,1},{8,14},{9,15},{10,... | collective-permute-start | bytes 1572872 | tf_op jit(solution)/shard_map/ppermute | solution.py:335
  267.8 57.4 %collective-permute-start.24 = (bf16[32,16,512]{2,1,0:T(8,128)(2,1)S(1)}, bf16[32,16,512]{2,1,0:T(8,128)(2,1)S(1)}, u32[]{:S(2)}, u32[]{:S(2)}) collective-permute-start(bf16[32,16,512]{2,1,0:T(8,128)(2,1)S(1)} %copy-done.64), channel_id=1, source_target_pairs={{15,9},{14,8},{13,11},{12,10},{11,13},{10,12},{9,15},{8,14},{31,25... | collective-permute-start | bytes 1572872 | tf_op jit(solution)/shard_map/ppermute | solution.py:335
  270.4 56.2 %collective-permute-start.29 = (bf16[16,32,512]{2,1,0:T(8,128)(2,1)S(1)}, bf16[16,32,512]{2,1,0:T(8,128)(2,1)S(1)}, u32[]{:S(2)}, u32[]{:S(2)}) collective-permute-start(bf16[16,32,512]{2,1,0:T(8,128)(2,1)S(1)} %copy-done.61), channel_id=1, source_target_pairs={{0,12},{1,13},{2,14},{3,15},{4,8},{5,9},{6,10},{7,11},{8,4},{9,5},... | collective-permute-start | bytes 1572872 | tf_op jit(solution)/shard_map/ppermute | solution.py:335
  288.6 70.4 %collective-permute-start.21 = (bf16[32,16,512]{2,1,0:T(8,128)(2,1)}, bf16[32,16,512]{2,1,0:T(8,128)(2,1)S(1)}, u32[]{:S(2)}, u32[]{:S(2)}) collective-permute-start(bf16[32,16,512]{2,1,0:T(8,128)(2,1)} %get-tuple-element.242), channel_id=1, source_target_pairs={{15,10},{14,11},{13,8},{12,9},{11,14},{10,15},{9,12},{8,13},{31,26... | collective-permute-start | bytes 1572872 | tf_op jit(solution)/shard_map/ppermute | solution.py:335
  293.8 65.1 %collective-permute-start.32 = (bf16[16,32,512]{2,1,0:T(8,128)(2,1)}, bf16[16,32,512]{2,1,0:T(8,128)(2,1)S(1)}, u32[]{:S(2)}, u32[]{:S(2)}) collective-permute-start(bf16[16,32,512]{2,1,0:T(8,128)(2,1)} %get-tuple-element.267), channel_id=1, source_target_pairs={{0,11},{1,10},{2,9},{3,8},{4,15},{5,14},{6,13},{7,12},{8,3},{9,2},... | collective-permute-start | bytes 1572872 | tf_op jit(solution)/shard_map/ppermute | solution.py:335
  314.0 67.4 %collective-permute-start.17 = (bf16[32,16,512]{2,1,0:T(8,128)(2,1)}, bf16[32,16,512]{2,1,0:T(8,128)(2,1)S(1)}, u32[]{:S(2)}, u32[]{:S(2)}) collective-permute-start(bf16[32,16,512]{2,1,0:T(8,128)(2,1)} %get-tuple-element.234), channel_id=1, source_target_pairs={{15,11},{14,10},{13,9},{12,8},{11,15},{10,14},{9,13},{8,12},{31,27... | collective-permute-start | bytes 1572872 | tf_op jit(solution)/shard_map/ppermute | solution.py:335
  325.2 56.3 %collective-permute-start.25 = (bf16[16,32,512]{2,1,0:T(8,128)(2,1)S(1)}, bf16[16,32,512]{2,1,0:T(8,128)(2,1)S(1)}, u32[]{:S(2)}, u32[]{:S(2)}) collective-permute-start(bf16[16,32,512]{2,1,0:T(8,128)(2,1)S(1)} %copy-done.60), channel_id=1, source_target_pairs={{0,13},{1,12},{2,15},{3,14},{4,9},{5,8},{6,11},{7,10},{8,5},{9,4},... | collective-permute-start | bytes 1572872 | tf_op jit(solution)/shard_map/ppermute | solution.py:335
  326.5 77.4 %collective-permute-start.30 = (bf16[16,32,512]{2,1,0:T(8,128)(2,1)}, bf16[16,32,512]{2,1,0:T(8,128)(2,1)S(1)}, u32[]{:S(2)}, u32[]{:S(2)}) collective-permute-start(bf16[16,32,512]{2,1,0:T(8,128)(2,1)} %get-tuple-element.261), channel_id=1, source_target_pairs={{0,4},{1,5},{2,6},{3,7},{4,0},{5,1},{6,2},{7,3},{8,12},{9,13},{10,... | collective-permute-start | bytes 1572872 | tf_op jit(solution)/shard_map/ppermute | solution.py:335
  359.0 47.7 %collective-permute-start.22 = (bf16[16,32,512]{2,1,0:T(8,128)(2,1)S(1)}, bf16[16,32,512]{2,1,0:T(8,128)(2,1)S(1)}, u32[]{:S(2)}, u32[]{:S(2)}) collective-permute-start(bf16[16,32,512]{2,1,0:T(8,128)(2,1)S(1)} %copy-done.59), channel_id=1, source_target_pairs={{0,14},{1,15},{2,12},{3,13},{4,10},{5,11},{6,8},{7,9},{8,6},{9,7},... | collective-permute-start | bytes 1572872 | tf_op jit(solution)/shard_map/ppermute | solution.py:335
  359.0 56.2 %collective-permute-start.33 = (bf16[16,32,512]{2,1,0:T(8,128)(2,1)}, bf16[16,32,512]{2,1,0:T(8,128)(2,1)S(1)}, u32[]{:S(2)}, u32[]{:S(2)}) collective-permute-start(bf16[16,32,512]{2,1,0:T(8,128)(2,1)} %get-tuple-element.268), channel_id=1, source_target_pairs={{0,5},{1,4},{2,7},{3,6},{4,1},{5,0},{6,3},{7,2},{8,13},{9,12},{10,... | collective-permute-start | bytes 1572872 | tf_op jit(solution)/shard_map/ppermute | solution.py:335
  381.4 36.7 %collective-permute-start.18 = (bf16[16,32,512]{2,1,0:T(8,128)(2,1)}, bf16[16,32,512]{2,1,0:T(8,128)(2,1)S(1)}, u32[]{:S(2)}, u32[]{:S(2)}) collective-permute-start(bf16[16,32,512]{2,1,0:T(8,128)(2,1)} %get-tuple-element.235), channel_id=1, source_target_pairs={{0,15},{1,14},{2,13},{3,12},{4,11},{5,10},{6,9},{7,8},{8,7},{9,6},... | collective-permute-start | bytes 1572872 | tf_op jit(solution)/shard_map/ppermute | solution.py:335
  381.5 37.0 %collective-permute-start.26 = (bf16[16,32,512]{2,1,0:T(8,128)(2,1)}, bf16[16,32,512]{2,1,0:T(8,128)(2,1)S(1)}, u32[]{:S(2)}, u32[]{:S(2)}) collective-permute-start(bf16[16,32,512]{2,1,0:T(8,128)(2,1)} %get-tuple-element.252), channel_id=1, source_target_pairs={{0,3},{1,2},{2,1},{3,0},{4,7},{5,6},{6,5},{7,4},{8,11},{9,10},{10,... | collective-permute-start | bytes 1572872 | tf_op jit(solution)/shard_map/ppermute | solution.py:335
  418.4 52.7 %collective-permute-start.42 = (bf16[32,16,512]{2,1,0:T(8,128)(2,1)}, bf16[32,16,512]{2,1,0:T(8,128)(2,1)S(1)}, u32[]{:S(2)}, u32[]{:S(2)}) collective-permute-start(bf16[32,16,512]{2,1,0:T(8,128)(2,1)} %get-tuple-element.302), channel_id=1, source_target_pairs={{15,14},{14,15},{13,12},{12,13},{11,10},{10,11},{9,8},{8,9},{31,30... | collective-permute-start | bytes 1572872 | tf_op jit(solution)/shard_map/ppermute | solution.py:335
  420.7 55.5 %collective-permute-start.45 = (bf16[32,16,512]{2,1,0:T(8,128)(2,1)}, bf16[32,16,512]{2,1,0:T(8,128)(2,1)S(1)}, u32[]{:S(2)}, u32[]{:S(2)}) collective-permute-start(bf16[32,16,512]{2,1,0:T(8,128)(2,1)} %get-tuple-element.309), channel_id=1, source_target_pairs={{15,1},{13,3},{11,5},{9,7},{7,9},{5,11},{3,13},{1,15},{31,17},{29,... | collective-permute-start | bytes 1572872 | tf_op jit(solution)/shard_map/ppermute | solution.py:335
  433.2 46.8 %collective-permute-start.47 = (bf16[32,16,512]{2,1,0:T(8,128)(2,1)}, bf16[32,16,512]{2,1,0:T(8,128)(2,1)S(1)}, u32[]{:S(2)}, u32[]{:S(2)}) collective-permute-start(bf16[32,16,512]{2,1,0:T(8,128)(2,1)} %get-tuple-element.318), channel_id=1, source_target_pairs={{15,2},{14,3},{11,6},{10,7},{7,10},{6,11},{3,14},{2,15},{31,18},{3... | collective-permute-start | bytes 1572872 | tf_op jit(solution)/shard_map/ppermute | solution.py:335
  476.3 55.9 %collective-permute-start.46 = (bf16[32,16,512]{2,1,0:T(8,128)(2,1)}, bf16[32,16,512]{2,1,0:T(8,128)(2,1)S(1)}, u32[]{:S(2)}, u32[]{:S(2)}) collective-permute-start(bf16[32,16,512]{2,1,0:T(8,128)(2,1)} %get-tuple-element.310), channel_id=1, source_target_pairs={{15,9},{14,8},{13,11},{12,10},{11,13},{10,12},{9,15},{8,14},{31,25... | collective-permute-start | bytes 1572872 | tf_op jit(solution)/shard_map/ppermute | solution.py:335
  480.0 52.9 %collective-permute-start.48 = (bf16[32,16,512]{2,1,0:T(8,128)(2,1)}, bf16[32,16,512]{2,1,0:T(8,128)(2,1)S(1)}, u32[]{:S(2)}, u32[]{:S(2)}) collective-permute-start(bf16[32,16,512]{2,1,0:T(8,128)(2,1)} %get-tuple-element.323), channel_id=1, source_target_pairs={{15,5},{14,4},{13,7},{12,6},{7,13},{6,12},{5,15},{4,14},{31,21},{3... | collective-permute-start | bytes 1572872 | tf_op jit(solution)/shard_map/ppermute | solution.py:335
  480.7 54.2 %collective-permute-start.36 = (bf16[32,16,512]{2,1,0:T(8,128)(2,1)}, bf16[32,16,512]{2,1,0:T(8,128)(2,1)S(1)}, u32[]{:S(2)}, u32[]{:S(2)}) collective-permute-start(bf16[32,16,512]{2,1,0:T(8,128)(2,1)} %get-tuple-element.287), channel_id=1, source_target_pairs={{15,3},{14,2},{11,7},{10,6},{7,11},{6,10},{3,15},{2,14},{31,19},{3... | collective-permute-start | bytes 1572872 | tf_op jit(solution)/shard_map/ppermute | solution.py:335
  490.0 52.1 %collective-permute-start.49 = (bf16[32,16,512]{2,1,0:T(8,128)(2,1)}, bf16[32,16,512]{2,1,0:T(8,128)(2,1)S(1)}, u32[]{:S(2)}, u32[]{:S(2)}) collective-permute-start(bf16[32,16,512]{2,1,0:T(8,128)(2,1)} %get-tuple-element.326), channel_id=1, source_target_pairs={{15,6},{14,7},{13,4},{12,5},{7,14},{6,15},{5,12},{4,13},{31,22},{3... | collective-permute-start | bytes 1572872 | tf_op jit(solution)/shard_map/ppermute | solution.py:335
  490.7 76.7 %collective-permute-start.40 = (bf16[32,16,512]{2,1,0:T(8,128)(2,1)}, bf16[32,16,512]{2,1,0:T(8,128)(2,1)S(1)}, u32[]{:S(2)}, u32[]{:S(2)}) collective-permute-start(bf16[32,16,512]{2,1,0:T(8,128)(2,1)} %get-tuple-element.296), channel_id=1, source_target_pairs={{15,11},{14,10},{13,9},{12,8},{11,15},{10,14},{9,13},{8,12},{31,27... | collective-permute-start | bytes 1572872 | tf_op jit(solution)/shard_map/ppermute | solution.py:335
  532.2 37.1 %collective-permute-start.50 = (bf16[32,16,512]{2,1,0:T(8,128)(2,1)}, bf16[32,16,512]{2,1,0:T(8,128)(2,1)S(1)}, u32[]{:S(2)}, u32[]{:S(2)}) collective-permute-start(bf16[32,16,512]{2,1,0:T(8,128)(2,1)} %get-tuple-element.329), channel_id=1, source_target_pairs={{15,7},{14,6},{13,5},{12,4},{7,15},{6,14},{5,13},{4,12},{31,23},{3... | collective-permute-start | bytes 1572872 | tf_op jit(solution)/shard_map/ppermute | solution.py:335
  532.9 53.4 %collective-permute-start.51 = (bf16[32,16,512]{2,1,0:T(8,128)(2,1)}, bf16[32,16,512]{2,1,0:T(8,128)(2,1)S(1)}, u32[]{:S(2)}, u32[]{:S(2)}) collective-permute-start(bf16[32,16,512]{2,1,0:T(8,128)(2,1)} %get-tuple-element.340), channel_id=1, source_target_pairs={{15,12},{14,13},{13,14},{12,15},{11,8},{10,9},{9,10},{8,11},{31,28... | collective-permute-start | bytes 1572872 | tf_op jit(solution)/shard_map/ppermute | solution.py:335
  534.9 57.2 %collective-permute-start.37 = (bf16[32,16,512]{2,1,0:T(8,128)(2,1)}, bf16[32,16,512]{2,1,0:T(8,128)(2,1)S(1)}, u32[]{:S(2)}, u32[]{:S(2)}) collective-permute-start(bf16[32,16,512]{2,1,0:T(8,128)(2,1)} %get-tuple-element.288), channel_id=1, source_target_pairs={{15,10},{14,11},{13,8},{12,9},{11,14},{10,15},{9,12},{8,13},{31,26... | collective-permute-start | bytes 1572872 | tf_op jit(solution)/shard_map/ppermute | solution.py:335
  542.1 97.7 %collective-permute-start.52 = (bf16[32,16,512]{2,1,0:T(8,128)(2,1)}, bf16[32,16,512]{2,1,0:T(8,128)(2,1)S(1)}, u32[]{:S(2)}, u32[]{:S(2)}) collective-permute-start(bf16[32,16,512]{2,1,0:T(8,128)(2,1)} %get-tuple-element.343), channel_id=1, source_target_pairs={{15,13},{14,12},{13,15},{12,14},{11,9},{10,8},{9,11},{8,10},{31,29... | collective-permute-start | bytes 1572872 | tf_op jit(solution)/shard_map/ppermute | solution.py:335
  567.4 73.1 %collective-permute-start.41 = (bf16[32,16,512]{2,1,0:T(8,128)(2,1)}, bf16[32,16,512]{2,1,0:T(8,128)(2,1)S(1)}, u32[]{:S(2)}, u32[]{:S(2)}) collective-permute-start(bf16[32,16,512]{2,1,0:T(8,128)(2,1)} %get-tuple-element.297), channel_id=1, source_target_pairs={{15,1},{13,3},{11,5},{9,7},{7,9},{5,11},{3,13},{1,15},{31,17},{29,... | collective-permute-start | bytes 1572872 | tf_op jit(solution)/shard_map/ppermute | solution.py:335
  570.2 71.1 %collective-permute-start.53 = (bf16[32,16,512]{2,1,0:T(8,128)(2,1)}, bf16[32,16,512]{2,1,0:T(8,128)(2,1)S(1)}, u32[]{:S(2)}, u32[]{:S(2)}) collective-permute-start(bf16[32,16,512]{2,1,0:T(8,128)(2,1)} %get-tuple-element.346), channel_id=1, source_target_pairs={{15,14},{14,15},{13,12},{12,13},{11,10},{10,11},{9,8},{8,9},{31,30... | collective-permute-start | bytes 1572872 | tf_op jit(solution)/shard_map/ppermute | solution.py:335
  586.3 66.7 %collective-permute-start.54 = (bf16[32,16,512]{2,1,0:T(8,128)(2,1)}, bf16[32,16,512]{2,1,0:T(8,128)(2,1)S(1)}, u32[]{:S(2)}, u32[]{:S(2)}) collective-permute-start(bf16[32,16,512]{2,1,0:T(8,128)(2,1)} %get-tuple-element.351), channel_id=1, source_target_pairs={{15,2},{14,3},{11,6},{10,7},{7,10},{6,11},{3,14},{2,15},{31,18},{3... | collective-permute-start | bytes 1572872 | tf_op jit(solution)/shard_map/ppermute | solution.py:335
  592.1 45.4 %collective-permute-start.38 = (bf16[16,16,512]{2,1,0:T(8,128)(2,1)S(1)}, bf16[16,16,512]{2,1,0:T(8,128)(2,1)S(1)}, u32[]{:S(2)}, u32[]{:S(2)}) collective-permute-start(bf16[16,16,512]{2,1,0:T(8,128)(2,1)S(1)} %copy-done.70), channel_id=1, source_target_pairs={{15,0},{14,1},{13,2},{12,3},{11,4},{10,5},{9,6},{8,7},{7,8},{6,9},... | collective-permute-start | bytes 786440 | tf_op jit(solution)/shard_map/ppermute | solution.py:335
  637.5 58.4 %collective-permute-start.55 = (bf16[32,16,512]{2,1,0:T(8,128)(2,1)}, bf16[32,16,512]{2,1,0:T(8,128)(2,1)S(1)}, u32[]{:S(2)}, u32[]{:S(2)}) collective-permute-start(bf16[32,16,512]{2,1,0:T(8,128)(2,1)} %get-tuple-element.353), channel_id=1, source_target_pairs={{15,3},{14,2},{11,7},{10,6},{7,11},{6,10},{3,15},{2,14},{31,19},{3... | collective-permute-start | bytes 1572872 | tf_op jit(solution)/shard_map/ppermute | solution.py:335
  639.8 56.0 %collective-permute-start.56 = (bf16[32,16,512]{2,1,0:T(8,128)(2,1)}, bf16[32,16,512]{2,1,0:T(8,128)(2,1)S(1)}, u32[]{:S(2)}, u32[]{:S(2)}) collective-permute-start(bf16[32,16,512]{2,1,0:T(8,128)(2,1)} %get-tuple-element.354), channel_id=1, source_target_pairs={{15,4},{14,5},{13,6},{12,7},{7,12},{6,13},{5,14},{4,15},{31,20},{3... | collective-permute-start | bytes 1572872 | tf_op jit(solution)/shard_map/ppermute | solution.py:335
  640.5 55.3 %collective-permute-start.57 = (bf16[32,16,512]{2,1,0:T(8,128)(2,1)}, bf16[32,16,512]{2,1,0:T(8,128)(2,1)S(1)}, u32[]{:S(2)}, u32[]{:S(2)}) collective-permute-start(bf16[32,16,512]{2,1,0:T(8,128)(2,1)} %get-tuple-element.355), channel_id=1, source_target_pairs={{15,5},{14,4},{13,7},{12,6},{7,13},{6,12},{5,15},{4,14},{31,21},{3... | collective-permute-start | bytes 1572872 | tf_op jit(solution)/shard_map/ppermute | solution.py:335
  641.2 54.6 %collective-permute-start.58 = (bf16[32,16,512]{2,1,0:T(8,128)(2,1)}, bf16[32,16,512]{2,1,0:T(8,128)(2,1)S(1)}, u32[]{:S(2)}, u32[]{:S(2)}) collective-permute-start(bf16[32,16,512]{2,1,0:T(8,128)(2,1)} %get-tuple-element.356), channel_id=1, source_target_pairs={{15,6},{14,7},{13,4},{12,5},{7,14},{6,15},{5,12},{4,13},{31,22},{3... | collective-permute-start | bytes 1572872 | tf_op jit(solution)/shard_map/ppermute | solution.py:335
  653.0 42.9 %collective-permute-start.59 = (bf16[32,16,512]{2,1,0:T(8,128)(2,1)S(1)}, bf16[32,16,512]{2,1,0:T(8,128)(2,1)S(1)}, u32[]{:S(2)}, u32[]{:S(2)}) collective-permute-start(bf16[32,16,512]{2,1,0:T(8,128)(2,1)S(1)} %copy-done.58), channel_id=1, source_target_pairs={{15,7},{14,6},{13,5},{12,4},{7,15},{6,14},{5,13},{4,12},{31,23},{3... | collective-permute-start | bytes 1572872 | tf_op jit(solution)/shard_map/ppermute | solution.py:335
  (83 other events, 4587.1 us)
